TPU v7x, 32 devices: a whole 2x2x4 slice. The times are simulated.
32 devices in a mesh: row: 4 (over x, core), col: 4 (over z), depth: 2 (over y).
Axes of the slice: x: 2, y: 2, z: 4, core: 2. Of those that a mesh axis runs over, the one named last changes fastest.
Arguments:
- candidates: bfloat16 [4096, 512], P('row', ('col', 'depth')), may hold values from -6 to 6
- references: bfloat16 [16384, 512], P(('col', 'depth'), 'row'), may hold values from -6 to 6
- rates: float32 [16384], P(('col', 'depth')), may hold values from 0.15 to 1.5
Outputs:
- kernel: float32 [4096, 16384], P('row', ('col', 'depth'))
All inputs are finite; a program needn't handle non-finite values.
Results may differ from a plain program's by a relative error of at most 0.0003.
Values may be sent and summed in bfloat16 or wider, within the bound.
No kernel may reach another device: no remote copies, remote signals or barrier semaphores. Data moves between devices by JAX's collectives and lax.ppermute only.
A program may use at most 64 MiB of HBM per device.

v0:
```python
import jax
import jax.numpy as jnp
from jax import lax
from jax.sharding import PartitionSpec as P


def per_device(candidates, references, rates):
    paired = lax.all_gather(candidates, "depth", axis=1, tiled=True)
    panel = lax.all_gather(paired, "col", axis=1, tiled=True)
    width = panel.shape[1]
    cand_sq = jnp.sum(jnp.square(panel.astype(jnp.float32)), axis=1)
    ref_whole = lax.all_gather(references, "row", axis=1, tiled=True)
    gram = lax.dot_general(
        panel, ref_whole, (((1,), (1,)), ((), ())), preferred_element_type=jnp.float32
    )
    ref_sq = jnp.sum(jnp.square(ref_whole.astype(jnp.float32)), axis=1)
    distance = cand_sq[:, None] + ref_sq[None, :] - 2.0 * gram
    return jnp.exp(-rates[None, :] * distance / width)


def solution(mesh):
    placed = (P("row", ("col", "depth")), P(("col", "depth"), "row"), P(("col", "depth")))
    return jax.shard_map(
        per_device,
        mesh=mesh,
        in_specs=placed,
        out_specs=P("row", ("col", "depth")),
        check_vma=False,
    )
```

profile of v0, /device:TPU:0, one launch (start us, length us, event | category | flops | bytes accessed | tf_op | source)
XLA Modules:
  0.0 86.2 jit_solution(17966104002795301806)
XLA Ops:
  6.5 0.0 all-gather.3.cloned.1.call-start
  6.5 9.0 %all_gather.9 = bf16[1024,128]{0,1:T(8,128)(2,1)} all-gather(bf16[1024,64]{0,1:T(8,128)(2,1)} %param.3), channel_id=1, replica_groups=mesh['row'=4,'col'=4,'depth'=2] {'depth'}, dimensions={1}, use_global_device_ids=true | all-gather | bytes 393216 | tf_op jit(solution)/shard_map/all_gather | solution.py:8
  15.5 0.0 all-gather.3.cloned.1.call-update
  15.5 0.0 all-gather.5.cloned.1.call-start
  15.6 0.7 all-gather.5.cloned.1.call-update
  16.3 0.7 neg.4
  17.0 26.9 %all-gather.3.cloned.1.call-done = bf16[1024,512]{0,1:T(8,128)(2,1)} async-done(((bf16[1024,128]{0,1:T(8,128)(2,1)}), bf16[1024,512]{0,1:T(8,128)(2,1)}) %all-gather.3.cloned.1.call-update) | async-done | bytes 1048592 | tf_op jit(solution)/shard_map/all_gather | solution.py:9
  43.9 1.5 %multiply_reduce_fusion.1 = f32[1024]{0:T(1024)S(1)} fusion(bf16[1024,512]{0,1:T(8,128)(2,1)} %all-gather.3.cloned.1.call-done), kind=kLoop, calls=%fused_computation.2 | loop fusion | flops 1571840 | bytes 1052672 | tf_op jit(solution)/shard_map/reduce_sum | solution.py:11
  45.4 22.4 %all-gather.5.cloned.1.call-done = bf16[2048,512]{1,0:T(8,128)(2,1)} async-done(((bf16[2048,128]{1,0:T(8,128)(2,1)}), bf16[2048,512]{1,0:T(8,128)(2,1)}) %all-gather.5.cloned.1.call-update) | async-done | bytes 2097168 | tf_op jit(solution)/shard_map/all_gather | solution.py:12
  67.8 2.1 %multiply_reduce_fusion = f32[2048]{0:T(1024)S(1)} fusion(bf16[2048,512]{1,0:T(8,128)(2,1)} %all-gather.5.cloned.1.call-done), kind=kLoop, calls=%fused_computation.1 | loop fusion | flops 3143680 | bytes 2105344 | tf_op jit(solution)/shard_map/reduce_sum | solution.py:16
  69.9 9.5 %multiply_exponential_fusion = f32[1024,2048]{1,0:T(8,128)} fusion(bf16[1024,512]{0,1:T(8,128)(2,1)} %all-gather.3.cloned.1.call-done, bf16[2048,512]{1,0:T(8,128)(2,1)} %all-gather.5.cloned.1.call-done, f32[2048]{0:T(1024)S(1)} %multiply_reduce_fusion, f32[1024]{0:T(1024)S(1)} %multiply_reduce_fusion.1, f32[2048]{0:T(1024)S(1)} %neg.4), kind=kOutput, calls=%fused_computation | convolution fusion | flops 2157969408 | bytes 11554816 | tf_op jit(solution)/shard_map/dot_general | solution.py:13
Async XLA Ops:
  6.5 37.4 %all-gather.3.cloned.1.call-start = ((), (), s32[]{:S(2)}) async-start(), calls=%async_computation | async-start | bytes 1310720 | tf_op jit(solution)/shard_map/all_gather | solution.py:9
  15.5 52.3 %all-gather.5.cloned.1.call-start = ((), (), s32[]{:S(2)}) async-start(), calls=%async_computation.1 | async-start | bytes 2621440 | tf_op jit(solution)/shard_map/all_gather | solution.py:12
Sparse Core Ops, SparseCore 0:
  15.7 28.2 all-gather.2
  45.5 22.3 all-gather.4
where the time goes:
time: 86.5 us; the launch traced here: 86.2 us
  waiting for transfers between devices  50.1 us (58%)
  between operations  13.4 us (15%)
  matrix products  9.5 us (11%)
  blocking collectives  8.97 us (10%)
  other arithmetic  4.24 us (5%)
    all_gather x1, waiting for transfers between devices, per_device(): panel = lax.all_gather(paired, 'col', axis=1, tiled=True)  26.9 us
    all_gather x1, waiting for transfers between devices, per_device(): ref_whole = lax.all_gather(references, 'row', axis=1, tiled=True)  22.4 us
    dot_general x1, matrix products, per_device(): lax.dot_general(panel, ref_whole, (((1,), (1,)), ((), ())), preferred_ele...  9.5 us
    all_gather x1, blocking collectives, per_device(): paired = lax.all_gather(candidates, 'depth', axis=1, tiled=True)  8.97 us
    reduce_sum x1, other arithmetic, per_device(): ref_sq = jnp.sum(jnp.square(ref_whole.astype(jnp.float32)), axis=1)  2.07 us
  transfers between devices with their start and end apart: 2, of which 2 were waited for; matrix products, arithmetic and copies ran while one was open for 3% of the time, Pallas kernels for 0%

commit v1 on v0

v1 whole, which is shorter than its diff:
```python
import functools

import jax
import jax.numpy as jnp
from jax import lax
from jax.experimental import pallas as pl
from jax.experimental.pallas import tpu as pltpu
from jax.sharding import PartitionSpec as P

LOG2E = 1.4426950408889634


def swap(value, axis, size, bit):
    return lax.ppermute(value, axis, [(i, i ^ bit) for i in range(size)])


def similarity_kernel(place, *refs, n_cand, n_ref, width):
    cands, rows = refs[:n_cand], refs[n_cand : n_cand + n_ref]
    rates, out, panel, lhs, half_sq = refs[n_cand + n_ref :]
    feats = cands[0].shape[0]

    @pl.when(pl.program_id(0) == 0)
    def _():
        for s in range(n_cand):
            panel[pl.ds(pl.multiple_of(place[s] * feats, feats), feats), :] = cands[s][...]
        lhs[...] = panel[...].T
        wide = lhs[...].astype(jnp.float32)
        half_sq[...] = jnp.broadcast_to(
            0.5 * jnp.sum(wide * wide, axis=1, keepdims=True), half_sq.shape
        )

    rhs = [r[...] for r in rows]
    squares = sum(jnp.square(v.astype(jnp.float32)) for v in rhs)
    half_ref = 0.5 * jnp.sum(squares.T, axis=0, keepdims=True)
    scale = rates[...] * (2.0 * LOG2E / width)
    gram = lax.dot_general(
        lhs[...],
        jnp.concatenate(rhs, axis=1),
        (((1,), (1,)), ((), ())),
        preferred_element_type=jnp.float32,
    )
    half_cand = jnp.concatenate([half_sq[...]] * (gram.shape[1] // 128), axis=1)
    out[...] = jnp.exp2((gram - half_cand - half_ref) * scale)


def similarity(cands, rows, rates, place, block):
    feats, m = cands[0].shape
    n, ref_feats = rows[0].shape
    width = feats * len(cands)
    return pl.pallas_call(
        functools.partial(similarity_kernel, n_cand=len(cands), n_ref=len(rows), width=width),
        grid_spec=pltpu.PrefetchScalarGridSpec(
            num_scalar_prefetch=1,
            grid=(n // block,),
            in_specs=[pl.BlockSpec((feats, m), lambda j, _: (0, 0))] * len(cands)
            + [pl.BlockSpec((block, ref_feats), lambda j, _: (j, 0))] * len(rows)
            + [pl.BlockSpec((1, block), lambda j, _: (0, j))],
            out_specs=pl.BlockSpec((m, block), lambda j, _: (0, j)),
            scratch_shapes=[
                pltpu.VMEM((width, m), jnp.bfloat16),
                pltpu.VMEM((m, width), jnp.bfloat16),
                pltpu.VMEM((m, 128), jnp.float32),
            ],
        ),
        out_shape=jax.ShapeDtypeStruct((m, n), jnp.float32),
        compiler_params=pltpu.CompilerParams(vmem_limit_bytes=48 * 2**20),
        name="similarity",
    )(place, *cands, *rows, rates.reshape(1, n))


def per_device(candidates, references, rates, *, n_row, n_col, n_depth):
    far = swap(references, "row", n_row, 2)
    side = swap(references, "row", n_row, 1)
    own = candidates.T
    two = swap(own, "col", n_col, 2)
    one = swap(own, "col", n_col, 1)
    across = [swap(own, "depth", n_depth, 1)]
    two, one, across[0], side = lax.optimization_barrier((two, one, across[0], side))
    three = swap(two, "col", n_col, 1)
    across += [swap(block, "depth", n_depth, 1) for block in (one, two)]
    across.append(swap(three, "depth", n_depth, 1))
    far, across[1], across[2] = lax.optimization_barrier((far, across[1], across[2]))
    rows = [references, side, far, swap(far, "row", n_row, 1)]
    cands = [block for pair in zip((own, one, two, three), across) for block in pair]
    here = lax.axis_index("col") * n_depth + lax.axis_index("depth")
    held = here ^ jnp.arange(len(cands), dtype=jnp.int32)
    share = len(cands) // len(rows)
    place = ((held // share) ^ lax.axis_index("row")) * share + held % share
    return similarity(cands, rows, rates, place.astype(jnp.int32), 256)


def gathered(candidates, references, rates):
    panel = lax.all_gather(candidates, ("col", "depth"), axis=1, tiled=True)
    ref_whole = lax.all_gather(references, "row", axis=1, tiled=True)
    return similarity([panel.T], [ref_whole], rates, jnp.zeros((1,), jnp.int32), 256)


def solution(mesh):
    sizes = mesh.shape
    placed = (P("row", ("col", "depth")), P(("col", "depth"), "row"), P(("col", "depth")))
    small = sizes["row"] == 4 and sizes["col"] == 4 and sizes["depth"] == 2
    body = gathered
    if small:
        body = functools.partial(
            per_device, n_row=sizes["row"], n_col=sizes["col"], n_depth=sizes["depth"]
        )
    return jax.shard_map(
        body,
        mesh=mesh,
        in_specs=placed,
        out_specs=P("row", ("col", "depth")),
        check_vma=False,
    )
```

time: 86.5 us -> 42.8 us (0.49)
  waiting for transfers between devices: 50.1 us -> 20 us
  between operations: 13.4 us -> 0.02 us
  starting transfers between devices: 0.04 us -> 12.5 us
  matrix products: 9.5 us -> 0 us
  blocking collectives: 8.97 us -> 0 us
  Pallas kernels: 0 us -> 7.44 us
  other arithmetic: 4.24 us -> 0.01 us
  local copies, waits for them, and re-layouts: 0 us -> 2.64 us
    all_gather x2 -> x0, waiting for transfers between devices: 49.4 us -> none  [the longest x1 26.9 us: per_device(): panel = lax.all_gather(paired, 'col', axis=1, tiled=True)]
    ppermute x0 -> x10, waiting for transfers between devices: none -> 20 us  [swap(): return lax.ppermute(value, axis, [(i, i ^ bit) for i in range(size)])]
    ppermute x0 -> x10, starting transfers between devices: none -> 12.5 us  [swap(): return lax.ppermute(value, axis, [(i, i ^ bit) for i in range(size)])]
    dot_general x1 -> x0, matrix products: 9.5 us -> none  [per_device(): lax.dot_general(panel, ref_whole, (((1,), (1,)), ((), ())), preferred_ele...]
    all_gather x1 -> x0, blocking collectives: 8.97 us -> none  [per_device(): paired = lax.all_gather(candidates, 'depth', axis=1, tiled=True)]
    pallas_call x0 -> x1, Pallas kernels: none -> 7.44 us  [similarity(): pl.pallas_call(functools.partial(similarity_kernel, n_cand=len(cands), n_...]
    reduce_sum x2 -> x0, other arithmetic: 3.54 us -> none  [the longest x1 2.07 us: per_device(): ref_sq = jnp.sum(jnp.square(ref_whole.astype(jnp.float32)), axis=1)]
    unnamed x0 -> x6, local copies, waits for them, and re-layouts: none -> 2.64 us
  transfers between devices with their start and end apart: 2 -> 10, of which waited for: 2 -> 7; matrix products, arithmetic and copies ran while one was open for 3% -> 0% of each run, Pallas kernels for 0% -> 0%
where the time goes in v1:
time: 42.8 us; the launch traced here: 42.6 us
  waiting for transfers between devices  20 us (47%)
  starting transfers between devices  12.5 us (29%)
  Pallas kernels  7.44 us (17%)
  local copies, waits for them, and re-layouts  2.64 us (6%)
    ppermute x10, waiting for transfers between devices, swap(): return lax.ppermute(value, axis, [(i, i ^ bit) for i in range(size)])  20 us
    ppermute x10, starting transfers between devices, swap(): return lax.ppermute(value, axis, [(i, i ^ bit) for i in range(size)])  12.5 us
    pallas_call x1, Pallas kernels, similarity(): pl.pallas_call(functools.partial(similarity_kernel, n_cand=len(cands), n_...  7.44 us
    unnamed x6, local copies, waits for them, and re-layouts  2.64 us
  transfers between devices with their start and end apart: 10, of which 7 were waited for; matrix products, arithmetic and copies ran while one was open for 0% of the time, Pallas kernels for 0%

profile of v1, /device:TPU:0, one launch (start us, length us, event | category | flops | bytes accessed | tf_op | source)
XLA Modules:
  0.0 42.6 jit_solution(8140762687606070842)
XLA Ops:
  0.0 0.5 %collective-permute-start.3 = (bf16[2048,128]{1,0:T(8,128)(2,1)}, bf16[2048,128]{1,0:T(8,128)(2,1)S(1)}, u32[]{:S(2)}, u32[]{:S(2)}) collective-permute-start(bf16[2048,128]{1,0:T(8,128)(2,1)} %refs_8_.1), channel_id=1, source_target_pairs={{0,8},{8,0},{16,24},{24,16},{1,9},{9,1},{17,25},{25,17},{2,10},{10... | collective-permute-start | bytes 1572872 | tf_op jit(solution)/shard_map/ppermute | solution.py:14
  0.5 2.5 %collective-permute-start.4 = (bf16[2048,128]{1,0:T(8,128)(2,1)}, bf16[2048,128]{1,0:T(8,128)(2,1)S(1)}, u32[]{:S(2)}, u32[]{:S(2)}) collective-permute-start(bf16[2048,128]{1,0:T(8,128)(2,1)} %refs_8_.1), channel_id=1, source_target_pairs={{0,16},{8,24},{16,0},{24,8},{1,17},{9,25},{17,1},{25,9},{2,18},{10... | collective-permute-start | bytes 1572872 | tf_op jit(solution)/shard_map/ppermute | solution.py:14
  2.9 1.5 %collective-permute-start.2 = (bf16[64,1024]{1,0:T(8,128)(2,1)}, bf16[64,1024]{1,0:T(8,128)(2,1)S(1)}, u32[]{:S(2)}, u32[]{:S(2)}) collective-permute-start(bf16[64,1024]{1,0:T(8,128)(2,1)} %bitcast.2), channel_id=1, source_target_pairs={{0,1},{1,0},{2,3},{3,2},{4,5},{5,4},{6,7},{7,6},{8,9},{9,8},{10,11... | collective-permute-start | bytes 393224 | tf_op jit(solution)/shard_map/ppermute | solution.py:14
  4.5 1.6 %collective-permute-start.1 = (bf16[64,1024]{1,0:T(8,128)(2,1)}, bf16[64,1024]{1,0:T(8,128)(2,1)S(1)}, u32[]{:S(2)}, u32[]{:S(2)}) collective-permute-start(bf16[64,1024]{1,0:T(8,128)(2,1)} %bitcast.3), channel_id=1, source_target_pairs={{0,2},{2,0},{4,6},{6,4},{1,3},{3,1},{5,7},{7,5},{8,10},{10,8},{12,... | collective-permute-start | bytes 393224 | tf_op jit(solution)/shard_map/ppermute | solution.py:14
  6.0 2.6 %collective-permute-start = (bf16[64,1024]{1,0:T(8,128)(2,1)}, bf16[64,1024]{1,0:T(8,128)(2,1)S(1)}, u32[]{:S(2)}, u32[]{:S(2)}) collective-permute-start(bf16[64,1024]{1,0:T(8,128)(2,1)} %bitcast.4), channel_id=1, source_target_pairs={{0,4},{2,6},{4,0},{6,2},{1,5},{3,7},{5,1},{7,3},{8,12},{10,14},{12... | collective-permute-start | bytes 393224 | tf_op jit(solution)/shard_map/ppermute | solution.py:14
  8.6 0.2 collective-permute-done.2.refs_1_
  8.8 3.3 %collective-permute-done.1.refs_2_ = bf16[64,1024]{1,0:T(8,128)(2,1)S(1)} collective-permute-done((bf16[64,1024]{1,0:T(8,128)(2,1)}, bf16[64,1024]{1,0:T(8,128)(2,1)S(1)}, u32[]{:S(2)}, u32[]{:S(2)}) %collective-permute-start.1) | collective-permute-done | bytes 131104 | tf_op jit(solution)/shard_map/ppermute | solution.py:14
  12.1 3.0 %collective-permute-done.refs_4_ = bf16[64,1024]{1,0:T(8,128)(2,1)S(1)} collective-permute-done((bf16[64,1024]{1,0:T(8,128)(2,1)}, bf16[64,1024]{1,0:T(8,128)(2,1)S(1)}, u32[]{:S(2)}, u32[]{:S(2)}) %collective-permute-start) | collective-permute-done | bytes 131104 | tf_op jit(solution)/shard_map/ppermute | solution.py:14
  15.1 0.0 collective-permute-done.3.refs_9_
  15.1 0.5 %collective-permute-start.5 = (bf16[64,1024]{1,0:T(8,128)(2,1)S(1)}, bf16[64,1024]{1,0:T(8,128)(2,1)S(1)}, u32[]{:S(2)}, u32[]{:S(2)}) collective-permute-start(bf16[64,1024]{1,0:T(8,128)(2,1)S(1)} %collective-permute-done.1.refs_2_), channel_id=1, source_target_pairs={{0,1},{1,0},{2,3},{3,2},{4,5},{5,4},{6,7},{7,6},{8,9},{9,8},{10,11... | collective-permute-start | bytes 393224 | tf_op jit(solution)/shard_map/ppermute | solution.py:14
  15.6 1.5 %collective-permute-start.6 = (bf16[64,1024]{1,0:T(8,128)(2,1)S(1)}, bf16[64,1024]{1,0:T(8,128)(2,1)S(1)}, u32[]{:S(2)}, u32[]{:S(2)}) collective-permute-start(bf16[64,1024]{1,0:T(8,128)(2,1)S(1)} %collective-permute-done.refs_4_), channel_id=1, source_target_pairs={{0,1},{1,0},{2,3},{3,2},{4,5},{5,4},{6,7},{7,6},{8,9},{9,8},{10,11... | collective-permute-start | bytes 393224 | tf_op jit(solution)/shard_map/ppermute | solution.py:14
  17.1 0.0 collective-permute-done.4.refs_10_
  17.1 2.9 %collective-permute-done.5.refs_3_ = bf16[64,1024]{1,0:T(8,128)(2,1)S(1)} collective-permute-done((bf16[64,1024]{1,0:T(8,128)(2,1)S(1)}, bf16[64,1024]{1,0:T(8,128)(2,1)S(1)}, u32[]{:S(2)}, u32[]{:S(2)}) %collective-permute-start.5) | collective-permute-done | bytes 131104 | tf_op jit(solution)/shard_map/ppermute | solution.py:14
  20.1 1.4 %collective-permute-done.6.refs_5_ = bf16[64,1024]{1,0:T(8,128)(2,1)S(1)} collective-permute-done((bf16[64,1024]{1,0:T(8,128)(2,1)S(1)}, bf16[64,1024]{1,0:T(8,128)(2,1)S(1)}, u32[]{:S(2)}, u32[]{:S(2)}) %collective-permute-start.6) | collective-permute-done | bytes 131104 | tf_op jit(solution)/shard_map/ppermute | solution.py:14
  21.5 0.0 collective-permute-start.9
  21.5 1.3 %collective-permute-start.7 = (bf16[64,1024]{1,0:T(8,128)(2,1)S(1)}, bf16[64,1024]{1,0:T(8,128)(2,1)S(1)}, u32[]{:S(2)}, u32[]{:S(2)}) collective-permute-start(bf16[64,1024]{1,0:T(8,128)(2,1)S(1)} %collective-permute-done.refs_4_), channel_id=1, source_target_pairs={{0,2},{2,0},{4,6},{6,4},{1,3},{3,1},{5,7},{7,5},{8,10},{10,8},{12,... | collective-permute-start | bytes 393224 | tf_op jit(solution)/shard_map/ppermute | solution.py:14
  22.7 4.7 %collective-permute-done.7.refs_6_ = bf16[64,1024]{1,0:T(8,128)(2,1)S(1)} collective-permute-done((bf16[64,1024]{1,0:T(8,128)(2,1)S(1)}, bf16[64,1024]{1,0:T(8,128)(2,1)S(1)}, u32[]{:S(2)}, u32[]{:S(2)}) %collective-permute-start.7) | collective-permute-done | bytes 131104 | tf_op jit(solution)/shard_map/ppermute | solution.py:14
  27.4 0.6 %collective-permute-start.8 = (bf16[64,1024]{1,0:T(8,128)(2,1)S(1)}, bf16[64,1024]{1,0:T(8,128)(2,1)S(1)}, u32[]{:S(2)}, u32[]{:S(2)}) collective-permute-start(bf16[64,1024]{1,0:T(8,128)(2,1)S(1)} %collective-permute-done.7.refs_6_), channel_id=1, source_target_pairs={{0,1},{1,0},{2,3},{3,2},{4,5},{5,4},{6,7},{7,6},{8,9},{9,8},{10,11... | collective-permute-start | bytes 393224 | tf_op jit(solution)/shard_map/ppermute | solution.py:14
  28.0 4.5 %collective-permute-done.8.refs_7_ = bf16[64,1024]{1,0:T(8,128)(2,1)S(1)} collective-permute-done((bf16[64,1024]{1,0:T(8,128)(2,1)S(1)}, bf16[64,1024]{1,0:T(8,128)(2,1)S(1)}, u32[]{:S(2)}, u32[]{:S(2)}) %collective-permute-start.8) | collective-permute-done | bytes 131104 | tf_op jit(solution)/shard_map/ppermute | solution.py:14
  32.5 0.0 collective-permute-done.9.refs_11_
  32.5 0.0 copy-start
  32.5 1.0 %copy-done = bf16[2048,128]{1,0:T(8,128)(2,1)S(1)} copy-done((bf16[2048,128]{1,0:T(8,128)(2,1)S(1)}, bf16[2048,128]{1,0:T(8,128)(2,1)}, u32[]{:S(2)}) %copy-start) | copy-done | bytes 524312
  33.6 0.0 copy-start.1
  33.6 0.9 %copy-done.1 = bf16[1024,64]{0,1:T(8,128)(2,1)S(1)} copy-done((bf16[1024,64]{0,1:T(8,128)(2,1)S(1)}, bf16[1024,64]{0,1:T(8,128)(2,1)}, u32[]{:S(2)}) %copy-start.1) | copy-done | bytes 131096
  34.5 0.0 copy-start.2
  34.5 0.7 %copy-done.2 = f32[2048]{0:T(1024)S(1)} copy-done((f32[2048]{0:T(1024)S(1)}, f32[2048]{0:T(1024)}, u32[]{:S(2)}) %copy-start.2) | copy-done | bytes 8216
  35.2 7.4 %similarity.1 = f32[1024,2048]{1,0:T(8,128)} custom-call(s32[8]{0:T(128)S(1)} %fusion.place, bf16[64,1024]{1,0:T(8,128)(2,1)S(1)} %bitcast.5, bf16[64,1024]{1,0:T(8,128)(2,1)S(1)} %collective-permute-done.2.refs_1_, bf16[64,1024]{1,0:T(8,128)(2,1)S(1)} %collective-permute-done.1.refs_2_, bf16[64,1024]{1,0:T(8,128)(2,1)S(1)} %collective-permute-done.5.refs_3_, ...), custom_call_target="tpu_custom_call" | custom-call | tf_op jit(solution)/shard_map/similarity/pallas_call | solution.py:50
  (1 shorter events, 0.0 us)
Async XLA Ops:
  0.0 15.1 %collective-permute-start.3 = (bf16[2048,128]{1,0:T(8,128)(2,1)}, bf16[2048,128]{1,0:T(8,128)(2,1)S(1)}, u32[]{:S(2)}, u32[]{:S(2)}) collective-permute-start(bf16[2048,128]{1,0:T(8,128)(2,1)} %refs_8_.1), channel_id=1, source_target_pairs={{0,8},{8,0},{16,24},{24,16},{1,9},{9,1},{17,25},{25,17},{2,10},{10... | collective-permute-start | bytes 1572872 | tf_op jit(solution)/shard_map/ppermute | solution.py:14
  0.5 16.7 %collective-permute-start.4 = (bf16[2048,128]{1,0:T(8,128)(2,1)}, bf16[2048,128]{1,0:T(8,128)(2,1)S(1)}, u32[]{:S(2)}, u32[]{:S(2)}) collective-permute-start(bf16[2048,128]{1,0:T(8,128)(2,1)} %refs_8_.1), channel_id=1, source_target_pairs={{0,16},{8,24},{16,0},{24,8},{1,17},{9,25},{17,1},{25,9},{2,18},{10... | collective-permute-start | bytes 1572872 | tf_op jit(solution)/shard_map/ppermute | solution.py:14
  2.9 5.8 %collective-permute-start.2 = (bf16[64,1024]{1,0:T(8,128)(2,1)}, bf16[64,1024]{1,0:T(8,128)(2,1)S(1)}, u32[]{:S(2)}, u32[]{:S(2)}) collective-permute-start(bf16[64,1024]{1,0:T(8,128)(2,1)} %bitcast.2), channel_id=1, source_target_pairs={{0,1},{1,0},{2,3},{3,2},{4,5},{5,4},{6,7},{7,6},{8,9},{9,8},{10,11... | collective-permute-start | bytes 393224 | tf_op jit(solution)/shard_map/ppermute | solution.py:14
  4.5 7.7 %collective-permute-start.1 = (bf16[64,1024]{1,0:T(8,128)(2,1)}, bf16[64,1024]{1,0:T(8,128)(2,1)S(1)}, u32[]{:S(2)}, u32[]{:S(2)}) collective-permute-start(bf16[64,1024]{1,0:T(8,128)(2,1)} %bitcast.3), channel_id=1, source_target_pairs={{0,2},{2,0},{4,6},{6,4},{1,3},{3,1},{5,7},{7,5},{8,10},{10,8},{12,... | collective-permute-start | bytes 393224 | tf_op jit(solution)/shard_map/ppermute | solution.py:14
  6.0 9.1 %collective-permute-start = (bf16[64,1024]{1,0:T(8,128)(2,1)}, bf16[64,1024]{1,0:T(8,128)(2,1)S(1)}, u32[]{:S(2)}, u32[]{:S(2)}) collective-permute-start(bf16[64,1024]{1,0:T(8,128)(2,1)} %bitcast.4), channel_id=1, source_target_pairs={{0,4},{2,6},{4,0},{6,2},{1,5},{3,7},{5,1},{7,3},{8,12},{10,14},{12... | collective-permute-start | bytes 393224 | tf_op jit(solution)/shard_map/ppermute | solution.py:14
  15.1 5.0 %collective-permute-start.5 = (bf16[64,1024]{1,0:T(8,128)(2,1)S(1)}, bf16[64,1024]{1,0:T(8,128)(2,1)S(1)}, u32[]{:S(2)}, u32[]{:S(2)}) collective-permute-start(bf16[64,1024]{1,0:T(8,128)(2,1)S(1)} %collective-permute-done.1.refs_2_), channel_id=1, source_target_pairs={{0,1},{1,0},{2,3},{3,2},{4,5},{5,4},{6,7},{7,6},{8,9},{9,8},{10,11... | collective-permute-start | bytes 393224 | tf_op jit(solution)/shard_map/ppermute | solution.py:14
  15.6 5.9 %collective-permute-start.6 = (bf16[64,1024]{1,0:T(8,128)(2,1)S(1)}, bf16[64,1024]{1,0:T(8,128)(2,1)S(1)}, u32[]{:S(2)}, u32[]{:S(2)}) collective-permute-start(bf16[64,1024]{1,0:T(8,128)(2,1)S(1)} %collective-permute-done.refs_4_), channel_id=1, source_target_pairs={{0,1},{1,0},{2,3},{3,2},{4,5},{5,4},{6,7},{7,6},{8,9},{9,8},{10,11... | collective-permute-start | bytes 393224 | tf_op jit(solution)/shard_map/ppermute | solution.py:14
  21.5 11.0 %collective-permute-start.9 = (bf16[2048,128]{1,0:T(8,128)(2,1)S(1)}, bf16[2048,128]{1,0:T(8,128)(2,1)S(1)}, u32[]{:S(2)}, u32[]{:S(2)}) collective-permute-start(bf16[2048,128]{1,0:T(8,128)(2,1)S(1)} %collective-permute-done.4.refs_10_), channel_id=1, source_target_pairs={{0,8},{8,0},{16,24},{24,16},{1,9},{9,1},{17,25},{25,17},{2,10},{10... | collective-permute-start | bytes 1572872 | tf_op jit(solution)/shard_map/ppermute | solution.py:14
  21.5 5.9 %collective-permute-start.7 = (bf16[64,1024]{1,0:T(8,128)(2,1)S(1)}, bf16[64,1024]{1,0:T(8,128)(2,1)S(1)}, u32[]{:S(2)}, u32[]{:S(2)}) collective-permute-start(bf16[64,1024]{1,0:T(8,128)(2,1)S(1)} %collective-permute-done.refs_4_), channel_id=1, source_target_pairs={{0,2},{2,0},{4,6},{6,4},{1,3},{3,1},{5,7},{7,5},{8,10},{10,8},{12,... | collective-permute-start | bytes 393224 | tf_op jit(solution)/shard_map/ppermute | solution.py:14
  27.4 5.1 %collective-permute-start.8 = (bf16[64,1024]{1,0:T(8,128)(2,1)S(1)}, bf16[64,1024]{1,0:T(8,128)(2,1)S(1)}, u32[]{:S(2)}, u32[]{:S(2)}) collective-permute-start(bf16[64,1024]{1,0:T(8,128)(2,1)S(1)} %collective-permute-done.7.refs_6_), channel_id=1, source_target_pairs={{0,1},{1,0},{2,3},{3,2},{4,5},{5,4},{6,7},{7,6},{8,9},{9,8},{10,11... | collective-permute-start | bytes 393224 | tf_op jit(solution)/shard_map/ppermute | solution.py:14
  32.5 1.0 %copy-start = (bf16[2048,128]{1,0:T(8,128)(2,1)S(1)}, bf16[2048,128]{1,0:T(8,128)(2,1)}, u32[]{:S(2)}) copy-start(bf16[2048,128]{1,0:T(8,128)(2,1)} %refs_8_.1) | copy-start | bytes 1572868
  33.6 0.9 %copy-start.1 = (bf16[1024,64]{0,1:T(8,128)(2,1)S(1)}, bf16[1024,64]{0,1:T(8,128)(2,1)}, u32[]{:S(2)}) copy-start(bf16[1024,64]{0,1:T(8,128)(2,1)} %param.3) | copy-start | bytes 393220
  34.5 0.7 %copy-start.2 = (f32[2048]{0:T(1024)S(1)}, f32[2048]{0:T(1024)}, u32[]{:S(2)}) copy-start(f32[2048]{0:T(1024)} %param.5) | copy-start | bytes 24580

commit v2 on v0

v2 whole, which is shorter than its diff:
```python
import functools

import jax
import jax.numpy as jnp
from jax import lax
from jax.experimental import pallas as pl
from jax.experimental.pallas import tpu as pltpu
from jax.sharding import PartitionSpec as P

LOG2E = 1.4426950408889634
HBM = pl.BlockSpec(memory_space=pltpu.HBM)
VMEM = pl.BlockSpec(memory_space=pltpu.VMEM)
SMEM = pl.BlockSpec(memory_space=pltpu.SMEM)


def swap(value, axis, size, bit):
    return lax.ppermute(value, axis, [(i, i ^ bit) for i in range(size)])


def group(here, panel, same, other):
    feats = same.shape[0]
    panel[pl.ds(pl.multiple_of(here[1] * feats, feats), feats), :] = same[...]
    panel[pl.ds(pl.multiple_of((1 - here[1]) * feats, feats), feats), :] = other[...]
    return panel[...].T


def prepare_kernel(here, own, own_rows, rates, other, *refs, width):
    groups, rows = refs[:4], refs[4:7]
    lhs, squares, ordered, half_ref, scale, panel, own_block, rows0, rate, sems = refs[7:]
    copies = [
        pltpu.make_async_copy(own, own_block, sems.at[0]),
        pltpu.make_async_copy(own_rows, rows0, sems.at[1]),
        pltpu.make_async_copy(rates, rate, sems.at[2]),
    ]
    for copy in copies:
        copy.start()
    total = 0.0
    pairs = [(own_block, other), groups[0:2], groups[2:4]]
    for k in (1, 2, 0):
        if k == 0:
            copies[0].wait()
        piece = group(here, panel.at[k], *pairs[k])
        lhs[:, 128 * k : 128 * (k + 1)] = piece
        total += jnp.square(piece.astype(jnp.float32))
    squares[...] = total
    copies[1].wait()
    copies[2].wait()
    n = rows0.shape[0]
    slots = [rows0, *rows]
    step = 256
    for j in range(0, n, step):
        block = slice(j, j + step)
        total = 0.0
        for t in range(4):
            piece = slots[t][block, :]
            k = here[0] ^ t
            ordered[k, block, :] = piece
            total += jnp.square(piece.astype(jnp.float32))
        half_ref[:, block] = 0.5 * jnp.sum(total.T, axis=0, keepdims=True)
    scale[...] = rate[...] * (2.0 * LOG2E / width)


def finish_kernel(here, lhs, squares, ordered, half_ref, scale, same, other, out, panel, last, half_sq, result, sems, *, cols, tile):
    m, n = result.shape
    piece = group(here, panel, same, other)
    last[...] = piece
    total = squares[...] + jnp.square(piece.astype(jnp.float32))
    half_sq[...] = jnp.broadcast_to(0.5 * jnp.sum(total, axis=1, keepdims=True), half_sq.shape)
    sends = []
    for j in range(0, n, cols):
        block = slice(j, j + cols)
        rhs = jnp.concatenate([ordered[k, block, :] for k in range(4)], axis=1)
        for i in range(0, m, tile):
            part = slice(i, i + tile)
            gram = lax.dot_general(
                jnp.concatenate([lhs[part, :], last[part, :]], axis=1),
                rhs,
                (((1,), (1,)), ((), ())),
                preferred_element_type=jnp.float32,
            )
            half_cand = jnp.concatenate([half_sq[part, :]] * (cols // 128), axis=1)
            result[part, block] = jnp.exp2(
                (gram - half_cand - half_ref[:, block]) * scale[:, block]
            )
        sends.append(
            pltpu.make_async_copy(result.at[:, block], out.at[:, block], sems.at[j // cols])
        )
        sends[-1].start()
    for send in sends:
        send.wait()


def prepare(here, own, references, rates, other, groups, rows):
    feats, m = own.shape
    n = references.shape[0]
    stay = [
        pltpu.with_memory_space_constraint(v, pltpu.HBM)
        for v in (own, references, rates.reshape(1, n))
    ]
    return pl.pallas_call(
        functools.partial(prepare_kernel, width=8 * feats),
        in_specs=[SMEM] + [HBM] * 3 + [VMEM] * 8,
        out_specs=[VMEM] * 5,
        out_shape=[
            jax.ShapeDtypeStruct((m, 384), jnp.bfloat16),
            jax.ShapeDtypeStruct((m, 128), jnp.float32),
            jax.ShapeDtypeStruct((4, n, 128), jnp.bfloat16),
            jax.ShapeDtypeStruct((1, n), jnp.float32),
            jax.ShapeDtypeStruct((1, n), jnp.float32),
        ],
        scratch_shapes=[
            pltpu.VMEM((3, 128, m), jnp.bfloat16),
            pltpu.VMEM((feats, m), jnp.bfloat16),
            pltpu.VMEM(references.shape, jnp.bfloat16),
            pltpu.VMEM((1, n), jnp.float32),
            pltpu.SemaphoreType.DMA((3,)),
        ],
        compiler_params=pltpu.CompilerParams(vmem_limit_bytes=24 * 2**20),
        name="prepare",
    )(here, *stay, other, *groups, *rows)


def finish(here, prepared, same, other, cols=256, tile=256):
    m, n = prepared[0].shape[0], prepared[2].shape[1]
    return pl.pallas_call(
        functools.partial(finish_kernel, cols=cols, tile=tile),
        in_specs=[SMEM] + [VMEM] * 7,
        out_specs=HBM,
        out_shape=jax.ShapeDtypeStruct((m, n), jnp.float32),
        scratch_shapes=[
            pltpu.VMEM((128, m), jnp.bfloat16),
            pltpu.VMEM((m, 128), jnp.bfloat16),
            pltpu.VMEM((m, 128), jnp.float32),
            pltpu.VMEM((m, n), jnp.float32),
            pltpu.SemaphoreType.DMA((n // cols,)),
        ],
        compiler_params=pltpu.CompilerParams(vmem_limit_bytes=40 * 2**20),
        name="finish",
    )(here, *prepared, same, other)


def per_device(candidates, references, rates, *, n_row, n_col, n_depth):
    own = candidates.T
    two = swap(own, "col", n_col, 2)
    far = swap(references, "row", n_row, 2)
    one = swap(own, "col", n_col, 1)
    across = [swap(own, "depth", n_depth, 1)]
    two, one = lax.optimization_barrier((two, one))
    three = swap(two, "col", n_col, 1)
    across += [swap(block, "depth", n_depth, 1) for block in (one, two)]
    far, three, across[0], across[1], across[2] = lax.optimization_barrier(
        (far, three, across[0], across[1], across[2])
    )
    across.append(swap(three, "depth", n_depth, 1))
    side = swap(references, "row", n_row, 1)
    farside = swap(far, "row", n_row, 1)
    here = jnp.stack(
        [lax.axis_index("row") ^ lax.axis_index("col"), lax.axis_index("depth")]
    ).astype(jnp.int32)
    prepared = prepare(
        here, own, references, rates, across[0], (one, across[1], two, across[2]), (side, far, farside)
    )
    return finish(here, prepared, three, across[3])


def gathered(candidates, references, rates):
    panel = lax.all_gather(candidates, ("col", "depth"), axis=1, tiled=True)
    whole = lax.all_gather(references, "row", axis=1, tiled=True)
    gram = lax.dot_general(
        panel, whole, (((1,), (1,)), ((), ())), preferred_element_type=jnp.float32
    )
    cand_sq = jnp.sum(jnp.square(panel.astype(jnp.float32)), axis=1)
    ref_sq = jnp.sum(jnp.square(whole.astype(jnp.float32)), axis=1)
    distance = cand_sq[:, None] + ref_sq[None, :] - 2.0 * gram
    return jnp.exp(-rates[None, :] * distance / panel.shape[1])


def solution(mesh):
    sizes = mesh.shape
    placed = (P("row", ("col", "depth")), P(("col", "depth"), "row"), P(("col", "depth")))
    shape = {"n_row": sizes["row"], "n_col": sizes["col"], "n_depth": sizes["depth"]}

    def body(candidates, references, rates):
        if tuple(shape.values()) == (4, 4, 2) and references.shape[1] == 128:
            return per_device(candidates, references, rates, **shape)
        return gathered(candidates, references, rates)

    return jax.shard_map(
        body,
        mesh=mesh,
        in_specs=placed,
        out_specs=P("row", ("col", "depth")),
        check_vma=False,
    )
```

time: 86.5 us -> 30.7 us (0.35)
  waiting for transfers between devices: 50.1 us -> 11.1 us
  between operations: 13.4 us -> 0.02 us
  starting transfers between devices: 0.04 us -> 12.5 us
  matrix products: 9.5 us -> 0 us
  blocking collectives: 8.97 us -> 0 us
  Pallas kernels: 0 us -> 6.88 us
  other arithmetic: 4.24 us -> 0.07 us
    all_gather x2 -> x0, waiting for transfers between devices: 49.4 us -> none  [the longest x1 26.9 us: per_device(): panel = lax.all_gather(paired, 'col', axis=1, tiled=True)]
    ppermute x0 -> x10, starting transfers between devices: none -> 12.5 us  [swap(): return lax.ppermute(value, axis, [(i, i ^ bit) for i in range(size)])]
    ppermute x0 -> x10, waiting for transfers between devices: none -> 11.1 us  [swap(): return lax.ppermute(value, axis, [(i, i ^ bit) for i in range(size)])]
    dot_general x1 -> x0, matrix products: 9.5 us -> none  [per_device(): lax.dot_general(panel, ref_whole, (((1,), (1,)), ((), ())), preferred_ele...]
    all_gather x1 -> x0, blocking collectives: 8.97 us -> none  [per_device(): paired = lax.all_gather(candidates, 'depth', axis=1, tiled=True)]
    pallas_call x0 -> x2, Pallas kernels: none -> 6.88 us  [the longest x1 4.45 us: finish(): pl.pallas_call(functools.partial(finish_kernel, cols=cols, tile=tile), in...]
    reduce_sum x2 -> x0, other arithmetic: 3.54 us -> none  [the longest x1 2.07 us: per_device(): ref_sq = jnp.sum(jnp.square(ref_whole.astype(jnp.float32)), axis=1)]
  transfers between devices with their start and end apart: 2 -> 10, of which waited for: 2 -> 7; matrix products, arithmetic and copies ran while one was open for 3% -> 0% of each run, Pallas kernels for 0% -> 8%
where the time goes in v2:
time: 30.7 us; the launch traced here: 30.5 us
  starting transfers between devices  12.5 us (41%)
  waiting for transfers between devices  11.1 us (36%)
  Pallas kernels  6.88 us (22%)
    ppermute x10, starting transfers between devices, swap(): return lax.ppermute(value, axis, [(i, i ^ bit) for i in range(size)])  12.5 us
    ppermute x10, waiting for transfers between devices, swap(): return lax.ppermute(value, axis, [(i, i ^ bit) for i in range(size)])  11.1 us
    pallas_call x1, Pallas kernels, finish(): pl.pallas_call(functools.partial(finish_kernel, cols=cols, tile=tile), in...  4.45 us
    pallas_call x1, Pallas kernels, prepare(): pl.pallas_call(functools.partial(prepare_kernel, width=8 * feats), in_spe...  2.43 us
  transfers between devices with their start and end apart: 10, of which 7 were waited for; matrix products, arithmetic and copies ran while one was open for 0% of the time, Pallas kernels for 8%

profile of v2, /device:TPU:0, one launch (start us, length us, event | category | flops | bytes accessed | tf_op | source)
XLA Modules:
  0.0 30.5 jit_solution(15795030746921861809)
XLA Ops:
  0.0 2.9 %collective-permute-start = (bf16[2048,128]{1,0:T(8,128)(2,1)}, bf16[2048,128]{1,0:T(8,128)(2,1)S(1)}, u32[]{:S(2)}, u32[]{:S(2)}) collective-permute-start(bf16[2048,128]{1,0:T(8,128)(2,1)} %own_rows.1), channel_id=1, source_target_pairs={{0,16},{8,24},{16,0},{24,8},{1,17},{9,25},{17,1},{25,9},{2,18},{10... | collective-permute-start | bytes 1572872 | tf_op jit(solution)/shard_map/ppermute | solution.py:17
  2.9 1.6 %collective-permute-start.2 = (bf16[64,1024]{1,0:T(8,128)(2,1)}, bf16[64,1024]{1,0:T(8,128)(2,1)S(1)}, u32[]{:S(2)}, u32[]{:S(2)}) collective-permute-start(bf16[64,1024]{1,0:T(8,128)(2,1)} %bitcast.4), channel_id=1, source_target_pairs={{0,2},{2,0},{4,6},{6,4},{1,3},{3,1},{5,7},{7,5},{8,10},{10,8},{12,... | collective-permute-start | bytes 393224 | tf_op jit(solution)/shard_map/ppermute | solution.py:17
  4.5 2.6 %collective-permute-start.1 = (bf16[64,1024]{1,0:T(8,128)(2,1)}, bf16[64,1024]{1,0:T(8,128)(2,1)S(1)}, u32[]{:S(2)}, u32[]{:S(2)}) collective-permute-start(bf16[64,1024]{1,0:T(8,128)(2,1)} %bitcast.5), channel_id=1, source_target_pairs={{0,4},{2,6},{4,0},{6,2},{1,5},{3,7},{5,1},{7,3},{8,12},{10,14},{12... | collective-permute-start | bytes 393224 | tf_op jit(solution)/shard_map/ppermute | solution.py:17
  7.1 1.5 %collective-permute-start.4 = (bf16[64,1024]{1,0:T(8,128)(2,1)}, bf16[64,1024]{1,0:T(8,128)(2,1)S(1)}, u32[]{:S(2)}, u32[]{:S(2)}) collective-permute-start(bf16[64,1024]{1,0:T(8,128)(2,1)} %bitcast.6), channel_id=1, source_target_pairs={{0,1},{1,0},{2,3},{3,2},{4,5},{5,4},{6,7},{7,6},{8,9},{9,8},{10,11... | collective-permute-start | bytes 393224 | tf_op jit(solution)/shard_map/ppermute | solution.py:17
  8.6 1.2 %collective-permute-done.2.refs_0_ = bf16[64,1024]{1,0:T(8,128)(2,1)S(1)} collective-permute-done((bf16[64,1024]{1,0:T(8,128)(2,1)}, bf16[64,1024]{1,0:T(8,128)(2,1)S(1)}, u32[]{:S(2)}, u32[]{:S(2)}) %collective-permute-start.2) | collective-permute-done | bytes 131104 | tf_op jit(solution)/shard_map/ppermute | solution.py:17
  9.8 3.4 %collective-permute-done.1.refs_2_ = bf16[64,1024]{1,0:T(8,128)(2,1)S(1)} collective-permute-done((bf16[64,1024]{1,0:T(8,128)(2,1)}, bf16[64,1024]{1,0:T(8,128)(2,1)S(1)}, u32[]{:S(2)}, u32[]{:S(2)}) %collective-permute-start.1) | collective-permute-done | bytes 131104 | tf_op jit(solution)/shard_map/ppermute | solution.py:17
  13.2 1.5 %collective-permute-start.5 = (bf16[64,1024]{1,0:T(8,128)(2,1)S(1)}, bf16[64,1024]{1,0:T(8,128)(2,1)S(1)}, u32[]{:S(2)}, u32[]{:S(2)}) collective-permute-start(bf16[64,1024]{1,0:T(8,128)(2,1)S(1)} %collective-permute-done.2.refs_0_), channel_id=1, source_target_pairs={{0,1},{1,0},{2,3},{3,2},{4,5},{5,4},{6,7},{7,6},{8,9},{9,8},{10,11... | collective-permute-start | bytes 393224 | tf_op jit(solution)/shard_map/ppermute | solution.py:17
  14.7 0.5 %collective-permute-start.6 = (bf16[64,1024]{1,0:T(8,128)(2,1)S(1)}, bf16[64,1024]{1,0:T(8,128)(2,1)S(1)}, u32[]{:S(2)}, u32[]{:S(2)}) collective-permute-start(bf16[64,1024]{1,0:T(8,128)(2,1)S(1)} %collective-permute-done.1.refs_2_), channel_id=1, source_target_pairs={{0,1},{1,0},{2,3},{3,2},{4,5},{5,4},{6,7},{7,6},{8,9},{9,8},{10,11... | collective-permute-start | bytes 393224 | tf_op jit(solution)/shard_map/ppermute | solution.py:17
  15.2 0.3 %collective-permute-start.3 = (bf16[64,1024]{1,0:T(8,128)(2,1)S(1)}, bf16[64,1024]{1,0:T(8,128)(2,1)S(1)}, u32[]{:S(2)}, u32[]{:S(2)}) collective-permute-start(bf16[64,1024]{1,0:T(8,128)(2,1)S(1)} %collective-permute-done.1.refs_2_), channel_id=1, source_target_pairs={{0,2},{2,0},{4,6},{6,4},{1,3},{3,1},{5,7},{7,5},{8,10},{10,8},{12,... | collective-permute-start | bytes 393224 | tf_op jit(solution)/shard_map/ppermute | solution.py:17
  15.5 0.0 collective-permute-done.4.other
  15.5 0.0 collective-permute-start.7
  15.5 2.6 %collective-permute-done.5.refs_1_ = bf16[64,1024]{1,0:T(8,128)(2,1)S(1)} collective-permute-done((bf16[64,1024]{1,0:T(8,128)(2,1)S(1)}, bf16[64,1024]{1,0:T(8,128)(2,1)S(1)}, u32[]{:S(2)}, u32[]{:S(2)}) %collective-permute-start.5) | collective-permute-done | bytes 131104 | tf_op jit(solution)/shard_map/ppermute | solution.py:17
  18.1 1.5 %collective-permute-done.6.refs_3_ = bf16[64,1024]{1,0:T(8,128)(2,1)S(1)} collective-permute-done((bf16[64,1024]{1,0:T(8,128)(2,1)S(1)}, bf16[64,1024]{1,0:T(8,128)(2,1)S(1)}, u32[]{:S(2)}, u32[]{:S(2)}) %collective-permute-start.6) | collective-permute-done | bytes 131104 | tf_op jit(solution)/shard_map/ppermute | solution.py:17
  19.7 0.5 %collective-permute-done.3.same = bf16[64,1024]{1,0:T(8,128)(2,1)S(1)} collective-permute-done((bf16[64,1024]{1,0:T(8,128)(2,1)S(1)}, bf16[64,1024]{1,0:T(8,128)(2,1)S(1)}, u32[]{:S(2)}, u32[]{:S(2)}) %collective-permute-start.3) | collective-permute-done | bytes 131104 | tf_op jit(solution)/shard_map/ppermute | solution.py:17
  20.2 0.0 collective-permute-done.refs_5_
  20.2 0.0 collective-permute-start.8
  20.2 1.5 %collective-permute-start.9 = (bf16[64,1024]{1,0:T(8,128)(2,1)S(1)}, bf16[64,1024]{1,0:T(8,128)(2,1)S(1)}, u32[]{:S(2)}, u32[]{:S(2)}) collective-permute-start(bf16[64,1024]{1,0:T(8,128)(2,1)S(1)} %collective-permute-done.3.same), channel_id=1, source_target_pairs={{0,1},{1,0},{2,3},{3,2},{4,5},{5,4},{6,7},{7,6},{8,9},{9,8},{10,11... | collective-permute-start | bytes 393224 | tf_op jit(solution)/shard_map/ppermute | solution.py:17
  21.7 0.1 pad_add_fusion.here
  21.8 0.0 collective-permute-done.7.refs_4_
  21.8 0.3 %collective-permute-done.8.refs_6_ = bf16[2048,128]{1,0:T(8,128)(2,1)S(1)} collective-permute-done((bf16[2048,128]{1,0:T(8,128)(2,1)S(1)}, bf16[2048,128]{1,0:T(8,128)(2,1)S(1)}, u32[]{:S(2)}, u32[]{:S(2)}) %collective-permute-start.8) | collective-permute-done | bytes 524320 | tf_op jit(solution)/shard_map/ppermute | solution.py:17
  22.1 2.4 %prepare.1 = (bf16[1024,384]{1,0:T(8,128)(2,1)S(1)}, f32[1024,128]{1,0:T(8,128)S(1)}, bf16[4,2048,128]{2,1,0:T(8,128)(2,1)S(1)}, f32[1,2048]{1,0:T(1,128)S(1)}, f32[1,2048]{1,0:T(1,128)S(1)}) custom-call(s32[2]{0:T(128)S(1)} %pad_add_fusion.here, bf16[64,1024]{1,0:T(8,128)(2,1)} %bitcast.7, bf16[2048,128]{1,0:T(8,128)(2,1)} %own_rows.1, f32[1,2048]{1,0:T(1,128)} %bitcast.8, ...), custom_call_target="tpu_custom_call" | custom-call | tf_op jit(solution)/shard_map/prepare/pallas_call | solution.py:100
  24.5 1.6 %collective-permute-done.9.other = bf16[64,1024]{1,0:T(8,128)(2,1)S(1)} collective-permute-done((bf16[64,1024]{1,0:T(8,128)(2,1)S(1)}, bf16[64,1024]{1,0:T(8,128)(2,1)S(1)}, u32[]{:S(2)}, u32[]{:S(2)}) %collective-permute-start.9) | collective-permute-done | bytes 131104 | tf_op jit(solution)/shard_map/ppermute | solution.py:17
  26.1 4.5 %finish.1 = f32[1024,2048]{1,0:T(8,128)} custom-call(s32[2]{0:T(128)S(1)} %pad_add_fusion.here, bf16[1024,384]{1,0:T(8,128)(2,1)S(1)} %get-tuple-element.23.lhs, f32[1024,128]{1,0:T(8,128)S(1)} %get-tuple-element.24.squares, bf16[4,2048,128]{2,1,0:T(8,128)(2,1)S(1)} %get-tuple-element.25.ordered, f32[1,2048]{1,0:T(1,128)S(1)} %get-tuple-element.26.half_ref, ...), custom_call_target="tpu_custom_call" | custom-call | tf_op jit(solution)/shard_map/finish/pallas_call | solution.py:125
Async XLA Ops:
  0.0 20.2 %collective-permute-start = (bf16[2048,128]{1,0:T(8,128)(2,1)}, bf16[2048,128]{1,0:T(8,128)(2,1)S(1)}, u32[]{:S(2)}, u32[]{:S(2)}) collective-permute-start(bf16[2048,128]{1,0:T(8,128)(2,1)} %own_rows.1), channel_id=1, source_target_pairs={{0,16},{8,24},{16,0},{24,8},{1,17},{9,25},{17,1},{25,9},{2,18},{10... | collective-permute-start | bytes 1572872 | tf_op jit(solution)/shard_map/ppermute | solution.py:17
  2.9 6.8 %collective-permute-start.2 = (bf16[64,1024]{1,0:T(8,128)(2,1)}, bf16[64,1024]{1,0:T(8,128)(2,1)S(1)}, u32[]{:S(2)}, u32[]{:S(2)}) collective-permute-start(bf16[64,1024]{1,0:T(8,128)(2,1)} %bitcast.4), channel_id=1, source_target_pairs={{0,2},{2,0},{4,6},{6,4},{1,3},{3,1},{5,7},{7,5},{8,10},{10,8},{12,... | collective-permute-start | bytes 393224 | tf_op jit(solution)/shard_map/ppermute | solution.py:17
  4.5 8.7 %collective-permute-start.1 = (bf16[64,1024]{1,0:T(8,128)(2,1)}, bf16[64,1024]{1,0:T(8,128)(2,1)S(1)}, u32[]{:S(2)}, u32[]{:S(2)}) collective-permute-start(bf16[64,1024]{1,0:T(8,128)(2,1)} %bitcast.5), channel_id=1, source_target_pairs={{0,4},{2,6},{4,0},{6,2},{1,5},{3,7},{5,1},{7,3},{8,12},{10,14},{12... | collective-permute-start | bytes 393224 | tf_op jit(solution)/shard_map/ppermute | solution.py:17
  7.1 8.4 %collective-permute-start.4 = (bf16[64,1024]{1,0:T(8,128)(2,1)}, bf16[64,1024]{1,0:T(8,128)(2,1)S(1)}, u32[]{:S(2)}, u32[]{:S(2)}) collective-permute-start(bf16[64,1024]{1,0:T(8,128)(2,1)} %bitcast.6), channel_id=1, source_target_pairs={{0,1},{1,0},{2,3},{3,2},{4,5},{5,4},{6,7},{7,6},{8,9},{9,8},{10,11... | collective-permute-start | bytes 393224 | tf_op jit(solution)/shard_map/ppermute | solution.py:17
  13.2 5.0 %collective-permute-start.5 = (bf16[64,1024]{1,0:T(8,128)(2,1)S(1)}, bf16[64,1024]{1,0:T(8,128)(2,1)S(1)}, u32[]{:S(2)}, u32[]{:S(2)}) collective-permute-start(bf16[64,1024]{1,0:T(8,128)(2,1)S(1)} %collective-permute-done.2.refs_0_), channel_id=1, source_target_pairs={{0,1},{1,0},{2,3},{3,2},{4,5},{5,4},{6,7},{7,6},{8,9},{9,8},{10,11... | collective-permute-start | bytes 393224 | tf_op jit(solution)/shard_map/ppermute | solution.py:17
  14.7 5.0 %collective-permute-start.6 = (bf16[64,1024]{1,0:T(8,128)(2,1)S(1)}, bf16[64,1024]{1,0:T(8,128)(2,1)S(1)}, u32[]{:S(2)}, u32[]{:S(2)}) collective-permute-start(bf16[64,1024]{1,0:T(8,128)(2,1)S(1)} %collective-permute-done.1.refs_2_), channel_id=1, source_target_pairs={{0,1},{1,0},{2,3},{3,2},{4,5},{5,4},{6,7},{7,6},{8,9},{9,8},{10,11... | collective-permute-start | bytes 393224 | tf_op jit(solution)/shard_map/ppermute | solution.py:17
  15.2 5.0 %collective-permute-start.3 = (bf16[64,1024]{1,0:T(8,128)(2,1)S(1)}, bf16[64,1024]{1,0:T(8,128)(2,1)S(1)}, u32[]{:S(2)}, u32[]{:S(2)}) collective-permute-start(bf16[64,1024]{1,0:T(8,128)(2,1)S(1)} %collective-permute-done.1.refs_2_), channel_id=1, source_target_pairs={{0,2},{2,0},{4,6},{6,4},{1,3},{3,1},{5,7},{7,5},{8,10},{10,8},{12,... | collective-permute-start | bytes 393224 | tf_op jit(solution)/shard_map/ppermute | solution.py:17
  15.5 6.2 %collective-permute-start.7 = (bf16[2048,128]{1,0:T(8,128)(2,1)}, bf16[2048,128]{1,0:T(8,128)(2,1)S(1)}, u32[]{:S(2)}, u32[]{:S(2)}) collective-permute-start(bf16[2048,128]{1,0:T(8,128)(2,1)} %own_rows.1), channel_id=1, source_target_pairs={{0,8},{8,0},{16,24},{24,16},{1,9},{9,1},{17,25},{25,17},{2,10},{10... | collective-permute-start | bytes 1572872 | tf_op jit(solution)/shard_map/ppermute | solution.py:17
  20.2 1.9 %collective-permute-start.8 = (bf16[2048,128]{1,0:T(8,128)(2,1)S(1)}, bf16[2048,128]{1,0:T(8,128)(2,1)S(1)}, u32[]{:S(2)}, u32[]{:S(2)}) collective-permute-start(bf16[2048,128]{1,0:T(8,128)(2,1)S(1)} %collective-permute-done.refs_5_), channel_id=1, source_target_pairs={{0,8},{8,0},{16,24},{24,16},{1,9},{9,1},{17,25},{25,17},{2,10},{10... | collective-permute-start | bytes 1572872 | tf_op jit(solution)/shard_map/ppermute | solution.py:17
  20.2 5.9 %collective-permute-start.9 = (bf16[64,1024]{1,0:T(8,128)(2,1)S(1)}, bf16[64,1024]{1,0:T(8,128)(2,1)S(1)}, u32[]{:S(2)}, u32[]{:S(2)}) collective-permute-start(bf16[64,1024]{1,0:T(8,128)(2,1)S(1)} %collective-permute-done.3.same), channel_id=1, source_target_pairs={{0,1},{1,0},{2,3},{3,2},{4,5},{5,4},{6,7},{7,6},{8,9},{9,8},{10,11... | collective-permute-start | bytes 393224 | tf_op jit(solution)/shard_map/ppermute | solution.py:17

commit v3 on v2

v3 whole, which is shorter than its diff:
```python
import functools

import jax
import jax.numpy as jnp
from jax import lax
from jax.experimental import pallas as pl
from jax.experimental.pallas import tpu as pltpu
from jax.sharding import PartitionSpec as P

LOG2E = 1.4426950408889634
HBM = pl.BlockSpec(memory_space=pltpu.HBM)
VMEM = pl.BlockSpec(memory_space=pltpu.VMEM)
SMEM = pl.BlockSpec(memory_space=pltpu.SMEM)


def swap(value, axis, size, bit):
    return lax.ppermute(value, axis, [(i, i ^ bit) for i in range(size)])


def group(depth, panel, same, other):
    feats = same.shape[0]
    panel[pl.ds(pl.multiple_of(depth * feats, feats), feats), :] = same[...]
    panel[pl.ds(pl.multiple_of((1 - depth) * feats, feats), feats), :] = other[...]
    return panel[...].T


def square_sums(rows):
    total = sum(jnp.square(r.astype(jnp.float32)) for r in rows)
    return 0.5 * jnp.sum(total.T, axis=0, keepdims=True)


def prepare_kernel(here, own, own_rows, rates, other, *refs, width, step):
    groups, rows = refs[:4], refs[4:6]
    lhs, squares, rows0, half_ref, scale, panel, own_block, rate, sems = refs[6:]
    copies = [
        pltpu.make_async_copy(own, own_block, sems.at[0]),
        pltpu.make_async_copy(own_rows, rows0, sems.at[1]),
        pltpu.make_async_copy(rates, rate, sems.at[2]),
    ]
    for copy in copies:
        copy.start()
    total = 0.0
    pairs = [(own_block, other), groups[0:2], groups[2:4]]
    for k in (1, 2, 0):
        if k == 0:
            copies[0].wait()
        piece = group(here[1], panel.at[k], *pairs[k])
        lhs[here[0] ^ k] = piece
        total += jnp.square(piece.astype(jnp.float32))
    squares[...] = total
    copies[1].wait()
    copies[2].wait()
    for j in range(0, rows0.shape[0], step):
        block = slice(j, j + step)
        half_ref[:, block] = square_sums([r[block, :] for r in (rows0, *rows)])
    scale[...] = rate[...] * (2.0 * LOG2E / width)


def finish_kernel(
    here, lhs, squares, rows0, half_ref, scale, side, far, farside, same, other, out,
    panel, whole, half_sq, result, sems, *, cols, tile,
):
    m, n = result.shape
    for t in range(4):
        whole[t] = lhs[t]
    piece = group(here[1], panel, same, other)
    whole[here[0] ^ 3] = piece
    total = squares[...] + jnp.square(piece.astype(jnp.float32))
    half_sq[...] = jnp.broadcast_to(0.5 * jnp.sum(total, axis=1, keepdims=True), half_sq.shape)
    sends = []
    for j in range(0, n, cols):
        block = slice(j, j + cols)
        rhs = jnp.concatenate([r[block, :] for r in (rows0, side, far, farside)], axis=1)
        half = half_ref[:, block] + square_sums([farside[block, :]])
        for i in range(0, m, tile):
            part = slice(i, i + tile)
            gram = lax.dot_general(
                jnp.concatenate([whole[t, part, :] for t in range(4)], axis=1),
                rhs,
                (((1,), (1,)), ((), ())),
                preferred_element_type=jnp.float32,
            )
            half_cand = jnp.concatenate([half_sq[part, :]] * (cols // 128), axis=1)
            result[part, block] = jnp.exp2((gram - half_cand - half) * scale[:, block])
        sends.append(
            pltpu.make_async_copy(result.at[:, block], out.at[:, block], sems.at[j // cols])
        )
        sends[-1].start()
    for send in sends:
        send.wait()


def prepare(here, own, references, rates, other, groups, rows):
    feats, m = own.shape
    n = references.shape[0]
    stay = [
        pltpu.with_memory_space_constraint(v, pltpu.HBM)
        for v in (own, references, rates.reshape(1, n))
    ]
    return pl.pallas_call(
        functools.partial(prepare_kernel, width=8 * feats, step=256),
        in_specs=[SMEM] + [HBM] * 3 + [VMEM] * 7,
        out_specs=[VMEM] * 5,
        out_shape=[
            jax.ShapeDtypeStruct((4, m, 128), jnp.bfloat16),
            jax.ShapeDtypeStruct((m, 128), jnp.float32),
            jax.ShapeDtypeStruct(references.shape, jnp.bfloat16),
            jax.ShapeDtypeStruct((1, n), jnp.float32),
            jax.ShapeDtypeStruct((1, n), jnp.float32),
        ],
        scratch_shapes=[
            pltpu.VMEM((3, 128, m), jnp.bfloat16),
            pltpu.VMEM((feats, m), jnp.bfloat16),
            pltpu.VMEM((1, n), jnp.float32),
            pltpu.SemaphoreType.DMA((3,)),
        ],
        compiler_params=pltpu.CompilerParams(vmem_limit_bytes=24 * 2**20),
        name="prepare",
    )(here, *stay, other, *groups, *rows)


def finish(here, prepared, rows, same, other, cols=256, tile=256):
    m, n = prepared[1].shape[0], prepared[2].shape[0]
    return pl.pallas_call(
        functools.partial(finish_kernel, cols=cols, tile=tile),
        in_specs=[SMEM] + [VMEM] * 10,
        out_specs=HBM,
        out_shape=jax.ShapeDtypeStruct((m, n), jnp.float32),
        scratch_shapes=[
            pltpu.VMEM((128, m), jnp.bfloat16),
            pltpu.VMEM((4, m, 128), jnp.bfloat16),
            pltpu.VMEM((m, 128), jnp.float32),
            pltpu.VMEM((m, n), jnp.float32),
            pltpu.SemaphoreType.DMA((n // cols,)),
        ],
        compiler_params=pltpu.CompilerParams(vmem_limit_bytes=40 * 2**20),
        name="finish",
    )(here, *prepared, *rows, same, other)


def per_device(candidates, references, rates, *, n_row, n_col, n_depth):
    own = candidates.T
    far = swap(references, "row", n_row, 2)
    two = swap(own, "col", n_col, 2)
    side = swap(references, "row", n_row, 1)
    late, side = lax.optimization_barrier((own, side))
    one = swap(late, "col", n_col, 1)
    y0 = swap(late, "depth", n_depth, 1)
    y3 = lax.ppermute(late, ("col", "depth"), [(i, i ^ 7) for i in range(8)])
    two, one = lax.optimization_barrier((two, one))
    three = swap(two, "col", n_col, 1)
    y1 = swap(one, "depth", n_depth, 1)
    y2 = swap(two, "depth", n_depth, 1)
    far, y0, y1, y2, three, y3 = lax.optimization_barrier((far, y0, y1, y2, three, y3))
    farside = swap(far, "row", n_row, 1)
    across = [y0, y1, y2, y3]
    here = jnp.stack(
        [lax.axis_index("row") ^ lax.axis_index("col"), lax.axis_index("depth")]
    ).astype(jnp.int32)
    prepared = prepare(
        here, own, references, rates, across[0], (one, across[1], two, across[2]), (side, far)
    )
    return finish(here, prepared, (side, far, farside), three, across[3])


def gathered(candidates, references, rates):
    panel = lax.all_gather(candidates, ("col", "depth"), axis=1, tiled=True)
    whole = lax.all_gather(references, "row", axis=1, tiled=True)
    gram = lax.dot_general(
        panel, whole, (((1,), (1,)), ((), ())), preferred_element_type=jnp.float32
    )
    cand_sq = jnp.sum(jnp.square(panel.astype(jnp.float32)), axis=1)
    ref_sq = jnp.sum(jnp.square(whole.astype(jnp.float32)), axis=1)
    distance = cand_sq[:, None] + ref_sq[None, :] - 2.0 * gram
    return jnp.exp(-rates[None, :] * distance / panel.shape[1])


def solution(mesh):
    sizes = mesh.shape
    placed = (P("row", ("col", "depth")), P(("col", "depth"), "row"), P(("col", "depth")))
    shape = {"n_row": sizes["row"], "n_col": sizes["col"], "n_depth": sizes["depth"]}

    def body(candidates, references, rates):
        if tuple(shape.values()) == (4, 4, 2) and references.shape[1] == 128:
            return per_device(candidates, references, rates, **shape)
        return gathered(candidates, references, rates)

    return jax.shard_map(
        body,
        mesh=mesh,
        in_specs=placed,
        out_specs=P("row", ("col", "depth")),
        check_vma=False,
    )
```

time: 30.7 us -> 29.5 us (0.961)
  waiting for transfers between devices: 11.1 us -> 9.52 us
  starting transfers between devices: 12.5 us -> 13.1 us
    ppermute x10 -> x9, waiting for transfers between devices: 11.1 us -> 9.51 us  [swap(): return lax.ppermute(value, axis, [(i, i ^ bit) for i in range(size)])]
    ppermute x0 -> x1, starting transfers between devices: none -> 1.46 us  [per_device(): y3 = lax.ppermute(late, ('col', 'depth'), [(i, i ^ 7) for i in range(8)])]
    ppermute x10 -> x9, starting transfers between devices: 12.5 us -> 11.6 us  [swap(): return lax.ppermute(value, axis, [(i, i ^ bit) for i in range(size)])]
    pallas_call x1, Pallas kernels: 2.43 us -> 2.07 us  [prepare(): pl.pallas_call(functools.partial(prepare_kernel, width=8 * feats, step=25...]
  transfers between devices with their start and end apart: 10 -> 10, of which waited for: 7 -> 3; matrix products, arithmetic and copies ran while one was open for 0% -> 0% of each run, Pallas kernels for 8% -> 7%
where the time goes in v3:
time: 29.5 us; the launch traced here: 29.3 us
  starting transfers between devices  13.1 us (44%)
  waiting for transfers between devices  9.52 us (32%)
  Pallas kernels  6.62 us (22%)
    ppermute x9, starting transfers between devices, swap(): return lax.ppermute(value, axis, [(i, i ^ bit) for i in range(size)])  11.6 us
    ppermute x9, waiting for transfers between devices, swap(): return lax.ppermute(value, axis, [(i, i ^ bit) for i in range(size)])  9.51 us
    pallas_call x1, Pallas kernels, finish(): pl.pallas_call(functools.partial(finish_kernel, cols=cols, tile=tile), in...  4.55 us
    pallas_call x1, Pallas kernels, prepare(): pl.pallas_call(functools.partial(prepare_kernel, width=8 * feats, step=25...  2.07 us
    ppermute x1, starting transfers between devices, per_device(): y3 = lax.ppermute(late, ('col', 'depth'), [(i, i ^ 7) for i in range(8)])  1.46 us
  transfers between devices with their start and end apart: 10, of which 3 were waited for; matrix products, arithmetic and copies ran while one was open for 0% of the time, Pallas kernels for 7%

profile of v3, /device:TPU:0, one launch (start us, length us, event | category | flops | bytes accessed | tf_op | source)
XLA Modules:
  0.0 29.3 jit_solution(3067626721291376343)
XLA Ops:
  0.0 0.5 %collective-permute-start.1 = (bf16[2048,128]{1,0:T(8,128)(2,1)}, bf16[2048,128]{1,0:T(8,128)(2,1)S(1)}, u32[]{:S(2)}, u32[]{:S(2)}) collective-permute-start(bf16[2048,128]{1,0:T(8,128)(2,1)} %own_rows.1), channel_id=1, source_target_pairs={{0,8},{8,0},{16,24},{24,16},{1,9},{9,1},{17,25},{25,17},{2,10},{10... | collective-permute-start | bytes 1572872 | tf_op jit(solution)/shard_map/ppermute | solution.py:17
  0.5 2.5 %collective-permute-start = (bf16[2048,128]{1,0:T(8,128)(2,1)}, bf16[2048,128]{1,0:T(8,128)(2,1)S(1)}, u32[]{:S(2)}, u32[]{:S(2)}) collective-permute-start(bf16[2048,128]{1,0:T(8,128)(2,1)} %own_rows.1), channel_id=1, source_target_pairs={{0,16},{8,24},{16,0},{24,8},{1,17},{9,25},{17,1},{25,9},{2,18},{10... | collective-permute-start | bytes 1572872 | tf_op jit(solution)/shard_map/ppermute | solution.py:17
  2.9 2.6 %collective-permute-start.3 = (bf16[64,1024]{1,0:T(8,128)(2,1)}, bf16[64,1024]{1,0:T(8,128)(2,1)S(1)}, u32[]{:S(2)}, u32[]{:S(2)}) collective-permute-start(bf16[64,1024]{1,0:T(8,128)(2,1)} %bitcast.4), channel_id=1, source_target_pairs={{0,4},{2,6},{4,0},{6,2},{1,5},{3,7},{5,1},{7,3},{8,12},{10,14},{12... | collective-permute-start | bytes 393224 | tf_op jit(solution)/shard_map/ppermute | solution.py:17
  5.5 0.0 collective-permute-done.1.refs_4_.side
  5.5 1.6 %collective-permute-start.4 = (bf16[64,1024]{1,0:T(8,128)(2,1)}, bf16[64,1024]{1,0:T(8,128)(2,1)S(1)}, u32[]{:S(2)}, u32[]{:S(2)}) collective-permute-start(bf16[64,1024]{1,0:T(8,128)(2,1)} %bitcast.5), channel_id=1, source_target_pairs={{0,2},{2,0},{4,6},{6,4},{1,3},{3,1},{5,7},{7,5},{8,10},{10,8},{12,... | collective-permute-start | bytes 393224 | tf_op jit(solution)/shard_map/ppermute | solution.py:17
  7.1 1.5 %collective-permute-start.8 = (bf16[64,1024]{1,0:T(8,128)(2,1)}, bf16[64,1024]{1,0:T(8,128)(2,1)S(1)}, u32[]{:S(2)}, u32[]{:S(2)}) collective-permute-start(bf16[64,1024]{1,0:T(8,128)(2,1)} %bitcast.6), channel_id=1, source_target_pairs={{0,7},{1,6},{2,5},{3,4},{4,3},{5,2},{6,1},{7,0},{8,15},{9,14},{10,... | collective-permute-start | bytes 393224 | tf_op jit(solution)/shard_map/ppermute | solution.py:149
  8.6 0.5 %collective-permute-start.2 = (bf16[64,1024]{1,0:T(8,128)(2,1)}, bf16[64,1024]{1,0:T(8,128)(2,1)S(1)}, u32[]{:S(2)}, u32[]{:S(2)}) collective-permute-start(bf16[64,1024]{1,0:T(8,128)(2,1)} %bitcast.7), channel_id=1, source_target_pairs={{0,1},{1,0},{2,3},{3,2},{4,5},{5,4},{6,7},{7,6},{8,9},{9,8},{10,11... | collective-permute-start | bytes 393224 | tf_op jit(solution)/shard_map/ppermute | solution.py:17
  9.1 4.5 %collective-permute-done.3.refs_2_ = bf16[64,1024]{1,0:T(8,128)(2,1)S(1)} collective-permute-done((bf16[64,1024]{1,0:T(8,128)(2,1)}, bf16[64,1024]{1,0:T(8,128)(2,1)S(1)}, u32[]{:S(2)}, u32[]{:S(2)}) %collective-permute-start.3) | collective-permute-done | bytes 131104 | tf_op jit(solution)/shard_map/ppermute | solution.py:17
  13.5 0.0 collective-permute-done.4.refs_0_
  13.5 1.5 %collective-permute-start.5 = (bf16[64,1024]{1,0:T(8,128)(2,1)S(1)}, bf16[64,1024]{1,0:T(8,128)(2,1)S(1)}, u32[]{:S(2)}, u32[]{:S(2)}) collective-permute-start(bf16[64,1024]{1,0:T(8,128)(2,1)S(1)} %collective-permute-done.4.refs_0_), channel_id=1, source_target_pairs={{0,1},{1,0},{2,3},{3,2},{4,5},{5,4},{6,7},{7,6},{8,9},{9,8},{10,11... | collective-permute-start | bytes 393224 | tf_op jit(solution)/shard_map/ppermute | solution.py:17
  15.1 1.4 %collective-permute-start.7 = (bf16[64,1024]{1,0:T(8,128)(2,1)S(1)}, bf16[64,1024]{1,0:T(8,128)(2,1)S(1)}, u32[]{:S(2)}, u32[]{:S(2)}) collective-permute-start(bf16[64,1024]{1,0:T(8,128)(2,1)S(1)} %collective-permute-done.3.refs_2_), channel_id=1, source_target_pairs={{0,2},{2,0},{4,6},{6,4},{1,3},{3,1},{5,7},{7,5},{8,10},{10,8},{12,... | collective-permute-start | bytes 393224 | tf_op jit(solution)/shard_map/ppermute | solution.py:17
  16.4 0.0 collective-permute-done.refs_5_.far
  16.4 1.1 %collective-permute-start.6 = (bf16[64,1024]{1,0:T(8,128)(2,1)S(1)}, bf16[64,1024]{1,0:T(8,128)(2,1)S(1)}, u32[]{:S(2)}, u32[]{:S(2)}) collective-permute-start(bf16[64,1024]{1,0:T(8,128)(2,1)S(1)} %collective-permute-done.3.refs_2_), channel_id=1, source_target_pairs={{0,1},{1,0},{2,3},{3,2},{4,5},{5,4},{6,7},{7,6},{8,9},{9,8},{10,11... | collective-permute-start | bytes 393224 | tf_op jit(solution)/shard_map/ppermute | solution.py:17
  17.5 0.0 collective-permute-done.8.other
  17.5 0.0 collective-permute-done.2.other
  17.5 2.9 %collective-permute-done.5.refs_1_ = bf16[64,1024]{1,0:T(8,128)(2,1)S(1)} collective-permute-done((bf16[64,1024]{1,0:T(8,128)(2,1)S(1)}, bf16[64,1024]{1,0:T(8,128)(2,1)S(1)}, u32[]{:S(2)}, u32[]{:S(2)}) %collective-permute-start.5) | collective-permute-done | bytes 131104 | tf_op jit(solution)/shard_map/ppermute | solution.py:17
  20.4 0.0 collective-permute-done.7.same
  20.4 2.2 %collective-permute-done.6.refs_3_ = bf16[64,1024]{1,0:T(8,128)(2,1)S(1)} collective-permute-done((bf16[64,1024]{1,0:T(8,128)(2,1)S(1)}, bf16[64,1024]{1,0:T(8,128)(2,1)S(1)}, u32[]{:S(2)}, u32[]{:S(2)}) %collective-permute-start.6) | collective-permute-done | bytes 131104 | tf_op jit(solution)/shard_map/ppermute | solution.py:17
  22.6 0.0 collective-permute-start.9
  22.6 0.1 pad_add_fusion.here
  22.7 2.1 %prepare.1 = (bf16[4,1024,128]{2,1,0:T(8,128)(2,1)S(1)}, f32[1024,128]{1,0:T(8,128)S(1)}, bf16[2048,128]{1,0:T(8,128)(2,1)S(1)}, f32[1,2048]{1,0:T(1,128)S(1)}, f32[1,2048]{1,0:T(1,128)S(1)}) custom-call(s32[2]{0:T(128)S(1)} %pad_add_fusion.here, bf16[64,1024]{1,0:T(8,128)(2,1)} %bitcast.8, bf16[2048,128]{1,0:T(8,128)(2,1)} %own_rows.1, f32[1,2048]{1,0:T(1,128)} %bitcast.9, ...), custom_call_target="tpu_custom_call" | custom-call | tf_op jit(solution)/shard_map/prepare/pallas_call | solution.py:100
  24.7 0.0 collective-permute-done.9.farside
  24.7 4.5 %finish.1 = f32[1024,2048]{1,0:T(8,128)} custom-call(s32[2]{0:T(128)S(1)} %pad_add_fusion.here, bf16[4,1024,128]{2,1,0:T(8,128)(2,1)S(1)} %get-tuple-element.28.lhs, f32[1024,128]{1,0:T(8,128)S(1)} %get-tuple-element.29.squares, bf16[2048,128]{1,0:T(8,128)(2,1)S(1)} %get-tuple-element.30.rows0, f32[1,2048]{1,0:T(1,128)S(1)} %get-tuple-element.31.half_ref, ...), custom_call_target="tpu_custom_call" | custom-call | tf_op jit(solution)/shard_map/finish/pallas_call | solution.py:124
Async XLA Ops:
  0.0 5.5 %collective-permute-start.1 = (bf16[2048,128]{1,0:T(8,128)(2,1)}, bf16[2048,128]{1,0:T(8,128)(2,1)S(1)}, u32[]{:S(2)}, u32[]{:S(2)}) collective-permute-start(bf16[2048,128]{1,0:T(8,128)(2,1)} %own_rows.1), channel_id=1, source_target_pairs={{0,8},{8,0},{16,24},{24,16},{1,9},{9,1},{17,25},{25,17},{2,10},{10... | collective-permute-start | bytes 1572872 | tf_op jit(solution)/shard_map/ppermute | solution.py:17
  0.5 16.0 %collective-permute-start = (bf16[2048,128]{1,0:T(8,128)(2,1)}, bf16[2048,128]{1,0:T(8,128)(2,1)S(1)}, u32[]{:S(2)}, u32[]{:S(2)}) collective-permute-start(bf16[2048,128]{1,0:T(8,128)(2,1)} %own_rows.1), channel_id=1, source_target_pairs={{0,16},{8,24},{16,0},{24,8},{1,17},{9,25},{17,1},{25,9},{2,18},{10... | collective-permute-start | bytes 1572872 | tf_op jit(solution)/shard_map/ppermute | solution.py:17
  2.9 10.6 %collective-permute-start.3 = (bf16[64,1024]{1,0:T(8,128)(2,1)}, bf16[64,1024]{1,0:T(8,128)(2,1)S(1)}, u32[]{:S(2)}, u32[]{:S(2)}) collective-permute-start(bf16[64,1024]{1,0:T(8,128)(2,1)} %bitcast.4), channel_id=1, source_target_pairs={{0,4},{2,6},{4,0},{6,2},{1,5},{3,7},{5,1},{7,3},{8,12},{10,14},{12... | collective-permute-start | bytes 393224 | tf_op jit(solution)/shard_map/ppermute | solution.py:17
  5.5 8.0 %collective-permute-start.4 = (bf16[64,1024]{1,0:T(8,128)(2,1)}, bf16[64,1024]{1,0:T(8,128)(2,1)S(1)}, u32[]{:S(2)}, u32[]{:S(2)}) collective-permute-start(bf16[64,1024]{1,0:T(8,128)(2,1)} %bitcast.5), channel_id=1, source_target_pairs={{0,2},{2,0},{4,6},{6,4},{1,3},{3,1},{5,7},{7,5},{8,10},{10,8},{12,... | collective-permute-start | bytes 393224 | tf_op jit(solution)/shard_map/ppermute | solution.py:17
  7.1 10.4 %collective-permute-start.8 = (bf16[64,1024]{1,0:T(8,128)(2,1)}, bf16[64,1024]{1,0:T(8,128)(2,1)S(1)}, u32[]{:S(2)}, u32[]{:S(2)}) collective-permute-start(bf16[64,1024]{1,0:T(8,128)(2,1)} %bitcast.6), channel_id=1, source_target_pairs={{0,7},{1,6},{2,5},{3,4},{4,3},{5,2},{6,1},{7,0},{8,15},{9,14},{10,... | collective-permute-start | bytes 393224 | tf_op jit(solution)/shard_map/ppermute | solution.py:149
  8.6 9.0 %collective-permute-start.2 = (bf16[64,1024]{1,0:T(8,128)(2,1)}, bf16[64,1024]{1,0:T(8,128)(2,1)S(1)}, u32[]{:S(2)}, u32[]{:S(2)}) collective-permute-start(bf16[64,1024]{1,0:T(8,128)(2,1)} %bitcast.7), channel_id=1, source_target_pairs={{0,1},{1,0},{2,3},{3,2},{4,5},{5,4},{6,7},{7,6},{8,9},{9,8},{10,11... | collective-permute-start | bytes 393224 | tf_op jit(solution)/shard_map/ppermute | solution.py:17
  13.5 6.8 %collective-permute-start.5 = (bf16[64,1024]{1,0:T(8,128)(2,1)S(1)}, bf16[64,1024]{1,0:T(8,128)(2,1)S(1)}, u32[]{:S(2)}, u32[]{:S(2)}) collective-permute-start(bf16[64,1024]{1,0:T(8,128)(2,1)S(1)} %collective-permute-done.4.refs_0_), channel_id=1, source_target_pairs={{0,1},{1,0},{2,3},{3,2},{4,5},{5,4},{6,7},{7,6},{8,9},{9,8},{10,11... | collective-permute-start | bytes 393224 | tf_op jit(solution)/shard_map/ppermute | solution.py:17
  15.1 5.3 %collective-permute-start.7 = (bf16[64,1024]{1,0:T(8,128)(2,1)S(1)}, bf16[64,1024]{1,0:T(8,128)(2,1)S(1)}, u32[]{:S(2)}, u32[]{:S(2)}) collective-permute-start(bf16[64,1024]{1,0:T(8,128)(2,1)S(1)} %collective-permute-done.3.refs_2_), channel_id=1, source_target_pairs={{0,2},{2,0},{4,6},{6,4},{1,3},{3,1},{5,7},{7,5},{8,10},{10,8},{12,... | collective-permute-start | bytes 393224 | tf_op jit(solution)/shard_map/ppermute | solution.py:17
  16.4 6.1 %collective-permute-start.6 = (bf16[64,1024]{1,0:T(8,128)(2,1)S(1)}, bf16[64,1024]{1,0:T(8,128)(2,1)S(1)}, u32[]{:S(2)}, u32[]{:S(2)}) collective-permute-start(bf16[64,1024]{1,0:T(8,128)(2,1)S(1)} %collective-permute-done.3.refs_2_), channel_id=1, source_target_pairs={{0,1},{1,0},{2,3},{3,2},{4,5},{5,4},{6,7},{7,6},{8,9},{9,8},{10,11... | collective-permute-start | bytes 393224 | tf_op jit(solution)/shard_map/ppermute | solution.py:17
  22.6 2.2 %collective-permute-start.9 = (bf16[2048,128]{1,0:T(8,128)(2,1)S(1)}, bf16[2048,128]{1,0:T(8,128)(2,1)S(1)}, u32[]{:S(2)}, u32[]{:S(2)}) collective-permute-start(bf16[2048,128]{1,0:T(8,128)(2,1)S(1)} %collective-permute-done.refs_5_.far), channel_id=1, source_target_pairs={{0,8},{8,0},{16,24},{24,16},{1,9},{9,1},{17,25},{25,17},{2,10},{10... | collective-permute-start | bytes 1572872 | tf_op jit(solution)/shard_map/ppermute | solution.py:17

commit v4 on v3

--- a/solution.py
+++ b/solution.py
@@ -41,11 +41,12 @@
         copy.start()
     total = 0.0
     pairs = [(own_block, other), groups[0:2], groups[2:4]]
+    step_of = (0, 1, 3)
     for k in (1, 2, 0):
         if k == 0:
             copies[0].wait()
         piece = group(here[1], panel.at[k], *pairs[k])
-        lhs[here[0] ^ k] = piece
+        lhs[here[0] ^ step_of[k]] = piece
         total += jnp.square(piece.astype(jnp.float32))
     squares[...] = total
     copies[1].wait()
@@ -56,17 +57,21 @@
     scale[...] = rate[...] * (2.0 * LOG2E / width)
 
 
+def turn_kernel(here, squares, same, other, turned, half_sq, panel):
+    piece = group(here[1], panel, same, other)
+    turned[...] = piece
+    total = squares[...] + jnp.square(piece.astype(jnp.float32))
+    half_sq[...] = jnp.broadcast_to(0.5 * jnp.sum(total, axis=1, keepdims=True), half_sq.shape)
+
+
 def finish_kernel(
-    here, lhs, squares, rows0, half_ref, scale, side, far, farside, same, other, out,
-    panel, whole, half_sq, result, sems, *, cols, tile,
+    here, lhs, rows0, half_ref, scale, side, far, farside, turned, half_sq, out,
+    whole, result, sems, *, cols, tile,
 ):
     m, n = result.shape
     for t in range(4):
         whole[t] = lhs[t]
-    piece = group(here[1], panel, same, other)
-    whole[here[0] ^ 3] = piece
-    total = squares[...] + jnp.square(piece.astype(jnp.float32))
-    half_sq[...] = jnp.broadcast_to(0.5 * jnp.sum(total, axis=1, keepdims=True), half_sq.shape)
+    whole[here[0] ^ 2] = turned[...]
     sends = []
     for j in range(0, n, cols):
         block = slice(j, j + cols)
@@ -119,23 +124,38 @@
     )(here, *stay, other, *groups, *rows)
 
 
-def finish(here, prepared, rows, same, other, cols=256, tile=256):
-    m, n = prepared[1].shape[0], prepared[2].shape[0]
+def turn(here, squares, same, other):
+    m = squares.shape[0]
+    return pl.pallas_call(
+        turn_kernel,
+        in_specs=[SMEM] + [VMEM] * 3,
+        out_specs=[VMEM] * 2,
+        out_shape=[
+            jax.ShapeDtypeStruct((m, 128), jnp.bfloat16),
+            jax.ShapeDtypeStruct((m, 128), jnp.float32),
+        ],
+        scratch_shapes=[pltpu.VMEM((128, m), jnp.bfloat16)],
+        compiler_params=pltpu.CompilerParams(vmem_limit_bytes=8 * 2**20),
+        cost_estimate=pl.CostEstimate(flops=10000000000, bytes_accessed=4194304, transcendentals=0),
+        name="turn",
+    )(here, squares, same, other)
+
+
+def finish(here, prepared, rows, turned, cols=256, tile=256):
+    m, n = prepared[0].shape[1], prepared[1].shape[0]
     return pl.pallas_call(
         functools.partial(finish_kernel, cols=cols, tile=tile),
-        in_specs=[SMEM] + [VMEM] * 10,
+        in_specs=[SMEM] + [VMEM] * 9,
         out_specs=HBM,
         out_shape=jax.ShapeDtypeStruct((m, n), jnp.float32),
         scratch_shapes=[
-            pltpu.VMEM((128, m), jnp.bfloat16),
             pltpu.VMEM((4, m, 128), jnp.bfloat16),
-            pltpu.VMEM((m, 128), jnp.float32),
             pltpu.VMEM((m, n), jnp.float32),
             pltpu.SemaphoreType.DMA((n // cols,)),
         ],
         compiler_params=pltpu.CompilerParams(vmem_limit_bytes=40 * 2**20),
         name="finish",
-    )(here, *prepared, *rows, same, other)
+    )(here, *prepared, *rows, *turned)
 
 
 def per_device(candidates, references, rates, *, n_row, n_col, n_depth):
@@ -151,16 +171,17 @@
     three = swap(two, "col", n_col, 1)
     y1 = swap(one, "depth", n_depth, 1)
     y2 = swap(two, "depth", n_depth, 1)
-    far, y0, y1, y2, three, y3 = lax.optimization_barrier((far, y0, y1, y2, three, y3))
+    far, y0, y3 = lax.optimization_barrier((far, y0, y3))
     farside = swap(far, "row", n_row, 1)
-    across = [y0, y1, y2, y3]
+    y1, three = lax.optimization_barrier((y1, three))
     here = jnp.stack(
         [lax.axis_index("row") ^ lax.axis_index("col"), lax.axis_index("depth")]
     ).astype(jnp.int32)
-    prepared = prepare(
-        here, own, references, rates, across[0], (one, across[1], two, across[2]), (side, far)
+    lhs, squares, *prepared = prepare(
+        here, own, references, rates, y0, (one, y1, three, y3), (side, far)
     )
-    return finish(here, prepared, (side, far, farside), three, across[3])
+    turned = turn(here, squares, two, y2)
+    return finish(here, (lhs, *prepared), (side, far, farside), turned)
 
 
 def gathered(candidates, references, rates):

time: 29.5 us -> 28 us (0.949)
  waiting for transfers between devices: 9.52 us -> 7.33 us
  Pallas kernels: 6.62 us -> 7.36 us
    ppermute x9, waiting for transfers between devices: 9.51 us -> 7.33 us  [swap(): return lax.ppermute(value, axis, [(i, i ^ bit) for i in range(size)])]
    pallas_call x0 -> x1, Pallas kernels: none -> 0.84 us  [turn(): pl.pallas_call(turn_kernel, in_specs=[SMEM] + [VMEM] * 3, out_specs=[VMEM...]
  transfers between devices with their start and end apart: 10 -> 10, of which waited for: 3 -> 3; matrix products, arithmetic and copies ran while one was open for 0% -> 0% of each run, Pallas kernels for 7% -> 10%
where the time goes in v4:
time: 28 us; the launch traced here: 27.9 us
  starting transfers between devices  13.1 us (47%)
  Pallas kernels  7.36 us (26%)
  waiting for transfers between devices  7.33 us (26%)
    ppermute x9, starting transfers between devices, swap(): return lax.ppermute(value, axis, [(i, i ^ bit) for i in range(size)])  11.6 us
    ppermute x9, waiting for transfers between devices, swap(): return lax.ppermute(value, axis, [(i, i ^ bit) for i in range(size)])  7.33 us
    pallas_call x1, Pallas kernels, finish(): pl.pallas_call(functools.partial(finish_kernel, cols=cols, tile=tile), in...  4.44 us
    pallas_call x1, Pallas kernels, prepare(): pl.pallas_call(functools.partial(prepare_kernel, width=8 * feats, step=25...  2.07 us
    ppermute x1, starting transfers between devices, per_device(): y3 = lax.ppermute(late, ('col', 'depth'), [(i, i ^ 7) for i in range(8)])  1.46 us
    pallas_call x1, Pallas kernels, turn(): pl.pallas_call(turn_kernel, in_specs=[SMEM] + [VMEM] * 3, out_specs=[VMEM...  0.84 us
  transfers between devices with their start and end apart: 10, of which 3 were waited for; matrix products, arithmetic and copies ran while one was open for 0% of the time, Pallas kernels for 10%

profile of v4, /device:TPU:0, one launch (start us, length us, event | category | flops | bytes accessed | tf_op | source)
XLA Modules:
  0.0 27.9 jit_solution(230668499273757407)
XLA Ops:
  0.0 0.5 %collective-permute-start.1 = (bf16[2048,128]{1,0:T(8,128)(2,1)}, bf16[2048,128]{1,0:T(8,128)(2,1)S(1)}, u32[]{:S(2)}, u32[]{:S(2)}) collective-permute-start(bf16[2048,128]{1,0:T(8,128)(2,1)} %own_rows.1), channel_id=1, source_target_pairs={{0,8},{8,0},{16,24},{24,16},{1,9},{9,1},{17,25},{25,17},{2,10},{10... | collective-permute-start | bytes 1572872 | tf_op jit(solution)/shard_map/ppermute | solution.py:17
  0.5 2.5 %collective-permute-start = (bf16[2048,128]{1,0:T(8,128)(2,1)}, bf16[2048,128]{1,0:T(8,128)(2,1)S(1)}, u32[]{:S(2)}, u32[]{:S(2)}) collective-permute-start(bf16[2048,128]{1,0:T(8,128)(2,1)} %own_rows.1), channel_id=1, source_target_pairs={{0,16},{8,24},{16,0},{24,8},{1,17},{9,25},{17,1},{25,9},{2,18},{10... | collective-permute-start | bytes 1572872 | tf_op jit(solution)/shard_map/ppermute | solution.py:17
  2.9 2.6 %collective-permute-start.4 = (bf16[64,1024]{1,0:T(8,128)(2,1)}, bf16[64,1024]{1,0:T(8,128)(2,1)S(1)}, u32[]{:S(2)}, u32[]{:S(2)}) collective-permute-start(bf16[64,1024]{1,0:T(8,128)(2,1)} %bitcast.4), channel_id=1, source_target_pairs={{0,4},{2,6},{4,0},{6,2},{1,5},{3,7},{5,1},{7,3},{8,12},{10,14},{12... | collective-permute-start | bytes 393224 | tf_op jit(solution)/shard_map/ppermute | solution.py:17
  5.5 0.0 collective-permute-done.1.refs_4_.side
  5.5 1.6 %collective-permute-start.5 = (bf16[64,1024]{1,0:T(8,128)(2,1)}, bf16[64,1024]{1,0:T(8,128)(2,1)S(1)}, u32[]{:S(2)}, u32[]{:S(2)}) collective-permute-start(bf16[64,1024]{1,0:T(8,128)(2,1)} %bitcast.5), channel_id=1, source_target_pairs={{0,2},{2,0},{4,6},{6,4},{1,3},{3,1},{5,7},{7,5},{8,10},{10,8},{12,... | collective-permute-start | bytes 393224 | tf_op jit(solution)/shard_map/ppermute | solution.py:17
  7.1 1.5 %collective-permute-start.3 = (bf16[64,1024]{1,0:T(8,128)(2,1)}, bf16[64,1024]{1,0:T(8,128)(2,1)S(1)}, u32[]{:S(2)}, u32[]{:S(2)}) collective-permute-start(bf16[64,1024]{1,0:T(8,128)(2,1)} %bitcast.6), channel_id=1, source_target_pairs={{0,7},{1,6},{2,5},{3,4},{4,3},{5,2},{6,1},{7,0},{8,15},{9,14},{10,... | collective-permute-start | bytes 393224 | tf_op jit(solution)/shard_map/ppermute | solution.py:169
  8.6 0.5 %collective-permute-start.2 = (bf16[64,1024]{1,0:T(8,128)(2,1)}, bf16[64,1024]{1,0:T(8,128)(2,1)S(1)}, u32[]{:S(2)}, u32[]{:S(2)}) collective-permute-start(bf16[64,1024]{1,0:T(8,128)(2,1)} %bitcast.7), channel_id=1, source_target_pairs={{0,1},{1,0},{2,3},{3,2},{4,5},{5,4},{6,7},{7,6},{8,9},{9,8},{10,11... | collective-permute-start | bytes 393224 | tf_op jit(solution)/shard_map/ppermute | solution.py:17
  9.1 4.5 %collective-permute-done.4.same = bf16[64,1024]{1,0:T(8,128)(2,1)S(1)} collective-permute-done((bf16[64,1024]{1,0:T(8,128)(2,1)}, bf16[64,1024]{1,0:T(8,128)(2,1)S(1)}, u32[]{:S(2)}, u32[]{:S(2)}) %collective-permute-start.4) | collective-permute-done | bytes 131104 | tf_op jit(solution)/shard_map/ppermute | solution.py:17
  13.5 0.0 collective-permute-done.5.refs_0_
  13.5 1.5 %collective-permute-start.6 = (bf16[64,1024]{1,0:T(8,128)(2,1)S(1)}, bf16[64,1024]{1,0:T(8,128)(2,1)S(1)}, u32[]{:S(2)}, u32[]{:S(2)}) collective-permute-start(bf16[64,1024]{1,0:T(8,128)(2,1)S(1)} %collective-permute-done.5.refs_0_), channel_id=1, source_target_pairs={{0,1},{1,0},{2,3},{3,2},{4,5},{5,4},{6,7},{7,6},{8,9},{9,8},{10,11... | collective-permute-start | bytes 393224 | tf_op jit(solution)/shard_map/ppermute | solution.py:17
  15.1 1.4 %collective-permute-start.7 = (bf16[64,1024]{1,0:T(8,128)(2,1)S(1)}, bf16[64,1024]{1,0:T(8,128)(2,1)S(1)}, u32[]{:S(2)}, u32[]{:S(2)}) collective-permute-start(bf16[64,1024]{1,0:T(8,128)(2,1)S(1)} %collective-permute-done.4.same), channel_id=1, source_target_pairs={{0,2},{2,0},{4,6},{6,4},{1,3},{3,1},{5,7},{7,5},{8,10},{10,8},{12,... | collective-permute-start | bytes 393224 | tf_op jit(solution)/shard_map/ppermute | solution.py:17
  16.4 0.0 collective-permute-done.refs_5_.far
  16.4 1.1 %collective-permute-start.9 = (bf16[64,1024]{1,0:T(8,128)(2,1)S(1)}, bf16[64,1024]{1,0:T(8,128)(2,1)S(1)}, u32[]{:S(2)}, u32[]{:S(2)}) collective-permute-start(bf16[64,1024]{1,0:T(8,128)(2,1)S(1)} %collective-permute-done.4.same), channel_id=1, source_target_pairs={{0,1},{1,0},{2,3},{3,2},{4,5},{5,4},{6,7},{7,6},{8,9},{9,8},{10,11... | collective-permute-start | bytes 393224 | tf_op jit(solution)/shard_map/ppermute | solution.py:17
  17.5 0.1 pad_add_fusion.here
  17.6 0.0 collective-permute-done.3.refs_3_
  17.6 0.0 collective-permute-done.2.other
  17.6 0.0 collective-permute-start.8
  17.6 2.8 %collective-permute-done.6.refs_1_ = bf16[64,1024]{1,0:T(8,128)(2,1)S(1)} collective-permute-done((bf16[64,1024]{1,0:T(8,128)(2,1)S(1)}, bf16[64,1024]{1,0:T(8,128)(2,1)S(1)}, u32[]{:S(2)}, u32[]{:S(2)}) %collective-permute-start.6) | collective-permute-done | bytes 131104 | tf_op jit(solution)/shard_map/ppermute | solution.py:17
  20.4 0.0 collective-permute-done.7.refs_2_
  20.4 2.1 %prepare.1 = (bf16[4,1024,128]{2,1,0:T(8,128)(2,1)S(1)}, f32[1024,128]{1,0:T(8,128)S(1)}, bf16[2048,128]{1,0:T(8,128)(2,1)S(1)}, f32[1,2048]{1,0:T(1,128)S(1)}, f32[1,2048]{1,0:T(1,128)S(1)}) custom-call(s32[2]{0:T(128)S(1)} %pad_add_fusion.here, bf16[64,1024]{1,0:T(8,128)(2,1)} %bitcast.8, bf16[2048,128]{1,0:T(8,128)(2,1)} %own_rows.1, f32[1,2048]{1,0:T(1,128)} %bitcast.9, ...), custom_call_target="tpu_custom_call" | custom-call | tf_op jit(solution)/shard_map/prepare/pallas_call | solution.py:105
  22.5 0.1 collective-permute-done.9.other
  22.6 0.8 %turn.1 = (bf16[1024,128]{1,0:T(8,128)(2,1)S(1)}, f32[1024,128]{1,0:T(8,128)S(1)}) custom-call(s32[2]{0:T(128)S(1)} %pad_add_fusion.here, f32[1024,128]{1,0:T(8,128)S(1)} %get-tuple-element.34.squares, bf16[64,1024]{1,0:T(8,128)(2,1)S(1)} %collective-permute-done.4.same, bf16[64,1024]{1,0:T(8,128)(2,1)S(1)} %collective-permute-done.9.other), custom_call_target="tpu_custom_call" | custom-call | flops 10000000000 | bytes 4194304 | tf_op jit(solution)/shard_map/turn/pallas_call | solution.py:129
  23.4 0.0 collective-permute-done.8.farside
  23.4 4.4 %finish.1 = f32[1024,2048]{1,0:T(8,128)} custom-call(s32[2]{0:T(128)S(1)} %pad_add_fusion.here, bf16[4,1024,128]{2,1,0:T(8,128)(2,1)S(1)} %get-tuple-element.30.lhs, bf16[2048,128]{1,0:T(8,128)(2,1)S(1)} %get-tuple-element.31.rows0, f32[1,2048]{1,0:T(1,128)S(1)} %get-tuple-element.32.half_ref, f32[1,2048]{1,0:T(1,128)S(1)} %get-tuple-element.33.scale, ...), custom_call_target="tpu_custom_call" | custom-call | tf_op jit(solution)/shard_map/finish/pallas_call | solution.py:146
Async XLA Ops:
  0.0 5.5 %collective-permute-start.1 = (bf16[2048,128]{1,0:T(8,128)(2,1)}, bf16[2048,128]{1,0:T(8,128)(2,1)S(1)}, u32[]{:S(2)}, u32[]{:S(2)}) collective-permute-start(bf16[2048,128]{1,0:T(8,128)(2,1)} %own_rows.1), channel_id=1, source_target_pairs={{0,8},{8,0},{16,24},{24,16},{1,9},{9,1},{17,25},{25,17},{2,10},{10... | collective-permute-start | bytes 1572872 | tf_op jit(solution)/shard_map/ppermute | solution.py:17
  0.5 16.0 %collective-permute-start = (bf16[2048,128]{1,0:T(8,128)(2,1)}, bf16[2048,128]{1,0:T(8,128)(2,1)S(1)}, u32[]{:S(2)}, u32[]{:S(2)}) collective-permute-start(bf16[2048,128]{1,0:T(8,128)(2,1)} %own_rows.1), channel_id=1, source_target_pairs={{0,16},{8,24},{16,0},{24,8},{1,17},{9,25},{17,1},{25,9},{2,18},{10... | collective-permute-start | bytes 1572872 | tf_op jit(solution)/shard_map/ppermute | solution.py:17
  2.9 10.6 %collective-permute-start.4 = (bf16[64,1024]{1,0:T(8,128)(2,1)}, bf16[64,1024]{1,0:T(8,128)(2,1)S(1)}, u32[]{:S(2)}, u32[]{:S(2)}) collective-permute-start(bf16[64,1024]{1,0:T(8,128)(2,1)} %bitcast.4), channel_id=1, source_target_pairs={{0,4},{2,6},{4,0},{6,2},{1,5},{3,7},{5,1},{7,3},{8,12},{10,14},{12... | collective-permute-start | bytes 393224 | tf_op jit(solution)/shard_map/ppermute | solution.py:17
  5.5 8.0 %collective-permute-start.5 = (bf16[64,1024]{1,0:T(8,128)(2,1)}, bf16[64,1024]{1,0:T(8,128)(2,1)S(1)}, u32[]{:S(2)}, u32[]{:S(2)}) collective-permute-start(bf16[64,1024]{1,0:T(8,128)(2,1)} %bitcast.5), channel_id=1, source_target_pairs={{0,2},{2,0},{4,6},{6,4},{1,3},{3,1},{5,7},{7,5},{8,10},{10,8},{12,... | collective-permute-start | bytes 393224 | tf_op jit(solution)/shard_map/ppermute | solution.py:17
  7.1 10.5 %collective-permute-start.3 = (bf16[64,1024]{1,0:T(8,128)(2,1)}, bf16[64,1024]{1,0:T(8,128)(2,1)S(1)}, u32[]{:S(2)}, u32[]{:S(2)}) collective-permute-start(bf16[64,1024]{1,0:T(8,128)(2,1)} %bitcast.6), channel_id=1, source_target_pairs={{0,7},{1,6},{2,5},{3,4},{4,3},{5,2},{6,1},{7,0},{8,15},{9,14},{10,... | collective-permute-start | bytes 393224 | tf_op jit(solution)/shard_map/ppermute | solution.py:169
  8.6 9.0 %collective-permute-start.2 = (bf16[64,1024]{1,0:T(8,128)(2,1)}, bf16[64,1024]{1,0:T(8,128)(2,1)S(1)}, u32[]{:S(2)}, u32[]{:S(2)}) collective-permute-start(bf16[64,1024]{1,0:T(8,128)(2,1)} %bitcast.7), channel_id=1, source_target_pairs={{0,1},{1,0},{2,3},{3,2},{4,5},{5,4},{6,7},{7,6},{8,9},{9,8},{10,11... | collective-permute-start | bytes 393224 | tf_op jit(solution)/shard_map/ppermute | solution.py:17
  13.5 6.8 %collective-permute-start.6 = (bf16[64,1024]{1,0:T(8,128)(2,1)S(1)}, bf16[64,1024]{1,0:T(8,128)(2,1)S(1)}, u32[]{:S(2)}, u32[]{:S(2)}) collective-permute-start(bf16[64,1024]{1,0:T(8,128)(2,1)S(1)} %collective-permute-done.5.refs_0_), channel_id=1, source_target_pairs={{0,1},{1,0},{2,3},{3,2},{4,5},{5,4},{6,7},{7,6},{8,9},{9,8},{10,11... | collective-permute-start | bytes 393224 | tf_op jit(solution)/shard_map/ppermute | solution.py:17
  15.1 5.3 %collective-permute-start.7 = (bf16[64,1024]{1,0:T(8,128)(2,1)S(1)}, bf16[64,1024]{1,0:T(8,128)(2,1)S(1)}, u32[]{:S(2)}, u32[]{:S(2)}) collective-permute-start(bf16[64,1024]{1,0:T(8,128)(2,1)S(1)} %collective-permute-done.4.same), channel_id=1, source_target_pairs={{0,2},{2,0},{4,6},{6,4},{1,3},{3,1},{5,7},{7,5},{8,10},{10,8},{12,... | collective-permute-start | bytes 393224 | tf_op jit(solution)/shard_map/ppermute | solution.py:17
  16.4 6.1 %collective-permute-start.9 = (bf16[64,1024]{1,0:T(8,128)(2,1)S(1)}, bf16[64,1024]{1,0:T(8,128)(2,1)S(1)}, u32[]{:S(2)}, u32[]{:S(2)}) collective-permute-start(bf16[64,1024]{1,0:T(8,128)(2,1)S(1)} %collective-permute-done.4.same), channel_id=1, source_target_pairs={{0,1},{1,0},{2,3},{3,2},{4,5},{5,4},{6,7},{7,6},{8,9},{9,8},{10,11... | collective-permute-start | bytes 393224 | tf_op jit(solution)/shard_map/ppermute | solution.py:17
  17.6 5.8 %collective-permute-start.8 = (bf16[2048,128]{1,0:T(8,128)(2,1)S(1)}, bf16[2048,128]{1,0:T(8,128)(2,1)S(1)}, u32[]{:S(2)}, u32[]{:S(2)}) collective-permute-start(bf16[2048,128]{1,0:T(8,128)(2,1)S(1)} %collective-permute-done.refs_5_.far), channel_id=1, source_target_pairs={{0,8},{8,0},{16,24},{24,16},{1,9},{9,1},{17,25},{25,17},{2,10},{10... | collective-permute-start | bytes 1572872 | tf_op jit(solution)/shard_map/ppermute | solution.py:17

commit v5 on v4

--- a/solution.py
+++ b/solution.py
@@ -60,18 +60,20 @@
 def turn_kernel(here, squares, same, other, turned, half_sq, panel):
     piece = group(here[1], panel, same, other)
     turned[...] = piece
-    total = squares[...] + jnp.square(piece.astype(jnp.float32))
-    half_sq[...] = jnp.broadcast_to(0.5 * jnp.sum(total, axis=1, keepdims=True), half_sq.shape)
+    half_sq[...] = squares[...] + jnp.square(piece.astype(jnp.float32))
 
 
 def finish_kernel(
-    here, lhs, rows0, half_ref, scale, side, far, farside, turned, half_sq, out,
-    whole, result, sems, *, cols, tile,
+    here, lhs, rows0, half_ref, scale, side, far, farside, turned, squares, out,
+    whole, half_sq, result, sems, *, cols, tile,
 ):
     m, n = result.shape
     for t in range(4):
         whole[t] = lhs[t]
     whole[here[0] ^ 2] = turned[...]
+    half_sq[...] = jnp.broadcast_to(
+        0.5 * jnp.sum(squares[...], axis=1, keepdims=True), half_sq.shape
+    )
     sends = []
     for j in range(0, n, cols):
         block = slice(j, j + cols)
@@ -150,6 +152,7 @@
         out_shape=jax.ShapeDtypeStruct((m, n), jnp.float32),
         scratch_shapes=[
             pltpu.VMEM((4, m, 128), jnp.bfloat16),
+            pltpu.VMEM((m, 128), jnp.float32),
             pltpu.VMEM((m, n), jnp.float32),
             pltpu.SemaphoreType.DMA((n // cols,)),
         ],

time: 28 us -> 27.9 us (level)
  no operation moved by 1% of the time
where the time goes in v5:
time: 27.9 us; the launch traced here: 27.8 us
  starting transfers between devices  13.1 us (47%)
  waiting for transfers between devices  7.33 us (26%)
  Pallas kernels  7.23 us (26%)
    ppermute x9, starting transfers between devices, swap(): return lax.ppermute(value, axis, [(i, i ^ bit) for i in range(size)])  11.6 us
    ppermute x9, waiting for transfers between devices, swap(): return lax.ppermute(value, axis, [(i, i ^ bit) for i in range(size)])  7.33 us
    pallas_call x1, Pallas kernels, finish(): pl.pallas_call(functools.partial(finish_kernel, cols=cols, tile=tile), in...  4.47 us
    pallas_call x1, Pallas kernels, prepare(): pl.pallas_call(functools.partial(prepare_kernel, width=8 * feats, step=25...  2.07 us
    ppermute x1, starting transfers between devices, per_device(): y3 = lax.ppermute(late, ('col', 'depth'), [(i, i ^ 7) for i in range(8)])  1.46 us
    pallas_call x1, Pallas kernels, turn(): pl.pallas_call(turn_kernel, in_specs=[SMEM] + [VMEM] * 3, out_specs=[VMEM...  0.69 us
  transfers between devices with their start and end apart: 10, of which 3 were waited for; matrix products, arithmetic and copies ran while one was open for 0% of the time, Pallas kernels for 10%

profile of v5, /device:TPU:0, one launch (start us, length us, event | category | flops | bytes accessed | tf_op | source)
XLA Modules:
  0.0 27.8 jit_solution(2679105620542633599)
XLA Ops:
  0.0 0.5 %collective-permute-start.1 = (bf16[2048,128]{1,0:T(8,128)(2,1)}, bf16[2048,128]{1,0:T(8,128)(2,1)S(1)}, u32[]{:S(2)}, u32[]{:S(2)}) collective-permute-start(bf16[2048,128]{1,0:T(8,128)(2,1)} %own_rows.1), channel_id=1, source_target_pairs={{0,8},{8,0},{16,24},{24,16},{1,9},{9,1},{17,25},{25,17},{2,10},{10... | collective-permute-start | bytes 1572872 | tf_op jit(solution)/shard_map/ppermute | solution.py:17
  0.5 2.5 %collective-permute-start = (bf16[2048,128]{1,0:T(8,128)(2,1)}, bf16[2048,128]{1,0:T(8,128)(2,1)S(1)}, u32[]{:S(2)}, u32[]{:S(2)}) collective-permute-start(bf16[2048,128]{1,0:T(8,128)(2,1)} %own_rows.1), channel_id=1, source_target_pairs={{0,16},{8,24},{16,0},{24,8},{1,17},{9,25},{17,1},{25,9},{2,18},{10... | collective-permute-start | bytes 1572872 | tf_op jit(solution)/shard_map/ppermute | solution.py:17
  2.9 2.6 %collective-permute-start.4 = (bf16[64,1024]{1,0:T(8,128)(2,1)}, bf16[64,1024]{1,0:T(8,128)(2,1)S(1)}, u32[]{:S(2)}, u32[]{:S(2)}) collective-permute-start(bf16[64,1024]{1,0:T(8,128)(2,1)} %bitcast.4), channel_id=1, source_target_pairs={{0,4},{2,6},{4,0},{6,2},{1,5},{3,7},{5,1},{7,3},{8,12},{10,14},{12... | collective-permute-start | bytes 393224 | tf_op jit(solution)/shard_map/ppermute | solution.py:17
  5.5 0.0 collective-permute-done.1.refs_4_.side
  5.5 1.6 %collective-permute-start.5 = (bf16[64,1024]{1,0:T(8,128)(2,1)}, bf16[64,1024]{1,0:T(8,128)(2,1)S(1)}, u32[]{:S(2)}, u32[]{:S(2)}) collective-permute-start(bf16[64,1024]{1,0:T(8,128)(2,1)} %bitcast.5), channel_id=1, source_target_pairs={{0,2},{2,0},{4,6},{6,4},{1,3},{3,1},{5,7},{7,5},{8,10},{10,8},{12,... | collective-permute-start | bytes 393224 | tf_op jit(solution)/shard_map/ppermute | solution.py:17
  7.1 1.5 %collective-permute-start.3 = (bf16[64,1024]{1,0:T(8,128)(2,1)}, bf16[64,1024]{1,0:T(8,128)(2,1)S(1)}, u32[]{:S(2)}, u32[]{:S(2)}) collective-permute-start(bf16[64,1024]{1,0:T(8,128)(2,1)} %bitcast.6), channel_id=1, source_target_pairs={{0,7},{1,6},{2,5},{3,4},{4,3},{5,2},{6,1},{7,0},{8,15},{9,14},{10,... | collective-permute-start | bytes 393224 | tf_op jit(solution)/shard_map/ppermute | solution.py:172
  8.6 0.5 %collective-permute-start.2 = (bf16[64,1024]{1,0:T(8,128)(2,1)}, bf16[64,1024]{1,0:T(8,128)(2,1)S(1)}, u32[]{:S(2)}, u32[]{:S(2)}) collective-permute-start(bf16[64,1024]{1,0:T(8,128)(2,1)} %bitcast.7), channel_id=1, source_target_pairs={{0,1},{1,0},{2,3},{3,2},{4,5},{5,4},{6,7},{7,6},{8,9},{9,8},{10,11... | collective-permute-start | bytes 393224 | tf_op jit(solution)/shard_map/ppermute | solution.py:17
  9.1 4.5 %collective-permute-done.4.same = bf16[64,1024]{1,0:T(8,128)(2,1)S(1)} collective-permute-done((bf16[64,1024]{1,0:T(8,128)(2,1)}, bf16[64,1024]{1,0:T(8,128)(2,1)S(1)}, u32[]{:S(2)}, u32[]{:S(2)}) %collective-permute-start.4) | collective-permute-done | bytes 131104 | tf_op jit(solution)/shard_map/ppermute | solution.py:17
  13.5 0.0 collective-permute-done.5.refs_0_
  13.5 1.5 %collective-permute-start.6 = (bf16[64,1024]{1,0:T(8,128)(2,1)S(1)}, bf16[64,1024]{1,0:T(8,128)(2,1)S(1)}, u32[]{:S(2)}, u32[]{:S(2)}) collective-permute-start(bf16[64,1024]{1,0:T(8,128)(2,1)S(1)} %collective-permute-done.5.refs_0_), channel_id=1, source_target_pairs={{0,1},{1,0},{2,3},{3,2},{4,5},{5,4},{6,7},{7,6},{8,9},{9,8},{10,11... | collective-permute-start | bytes 393224 | tf_op jit(solution)/shard_map/ppermute | solution.py:17
  15.1 1.4 %collective-permute-start.7 = (bf16[64,1024]{1,0:T(8,128)(2,1)S(1)}, bf16[64,1024]{1,0:T(8,128)(2,1)S(1)}, u32[]{:S(2)}, u32[]{:S(2)}) collective-permute-start(bf16[64,1024]{1,0:T(8,128)(2,1)S(1)} %collective-permute-done.4.same), channel_id=1, source_target_pairs={{0,2},{2,0},{4,6},{6,4},{1,3},{3,1},{5,7},{7,5},{8,10},{10,8},{12,... | collective-permute-start | bytes 393224 | tf_op jit(solution)/shard_map/ppermute | solution.py:17
  16.4 0.0 collective-permute-done.refs_5_.far
  16.4 1.1 %collective-permute-start.9 = (bf16[64,1024]{1,0:T(8,128)(2,1)S(1)}, bf16[64,1024]{1,0:T(8,128)(2,1)S(1)}, u32[]{:S(2)}, u32[]{:S(2)}) collective-permute-start(bf16[64,1024]{1,0:T(8,128)(2,1)S(1)} %collective-permute-done.4.same), channel_id=1, source_target_pairs={{0,1},{1,0},{2,3},{3,2},{4,5},{5,4},{6,7},{7,6},{8,9},{9,8},{10,11... | collective-permute-start | bytes 393224 | tf_op jit(solution)/shard_map/ppermute | solution.py:17
  17.5 0.1 pad_add_fusion.here
  17.6 0.0 collective-permute-done.3.refs_3_
  17.6 0.0 collective-permute-done.2.other
  17.6 0.0 collective-permute-start.8
  17.6 2.8 %collective-permute-done.6.refs_1_ = bf16[64,1024]{1,0:T(8,128)(2,1)S(1)} collective-permute-done((bf16[64,1024]{1,0:T(8,128)(2,1)S(1)}, bf16[64,1024]{1,0:T(8,128)(2,1)S(1)}, u32[]{:S(2)}, u32[]{:S(2)}) %collective-permute-start.6) | collective-permute-done | bytes 131104 | tf_op jit(solution)/shard_map/ppermute | solution.py:17
  20.4 0.0 collective-permute-done.7.refs_2_
  20.4 2.1 %prepare.1 = (bf16[4,1024,128]{2,1,0:T(8,128)(2,1)S(1)}, f32[1024,128]{1,0:T(8,128)S(1)}, bf16[2048,128]{1,0:T(8,128)(2,1)S(1)}, f32[1,2048]{1,0:T(1,128)S(1)}, f32[1,2048]{1,0:T(1,128)S(1)}) custom-call(s32[2]{0:T(128)S(1)} %pad_add_fusion.here, bf16[64,1024]{1,0:T(8,128)(2,1)} %bitcast.8, bf16[2048,128]{1,0:T(8,128)(2,1)} %own_rows.1, f32[1,2048]{1,0:T(1,128)} %bitcast.9, ...), custom_call_target="tpu_custom_call" | custom-call | tf_op jit(solution)/shard_map/prepare/pallas_call | solution.py:107
  22.5 0.1 collective-permute-done.9.other
  22.6 0.7 %turn.1 = (bf16[1024,128]{1,0:T(8,128)(2,1)S(1)}, f32[1024,128]{1,0:T(8,128)S(1)}) custom-call(s32[2]{0:T(128)S(1)} %pad_add_fusion.here, f32[1024,128]{1,0:T(8,128)S(1)} %get-tuple-element.34.squares, bf16[64,1024]{1,0:T(8,128)(2,1)S(1)} %collective-permute-done.4.same, bf16[64,1024]{1,0:T(8,128)(2,1)S(1)} %collective-permute-done.9.other), custom_call_target="tpu_custom_call" | custom-call | flops 10000000000 | bytes 4194304 | tf_op jit(solution)/shard_map/turn/pallas_call | solution.py:131
  23.3 0.0 collective-permute-done.8.farside
  23.3 4.5 %finish.1 = f32[1024,2048]{1,0:T(8,128)} custom-call(s32[2]{0:T(128)S(1)} %pad_add_fusion.here, bf16[4,1024,128]{2,1,0:T(8,128)(2,1)S(1)} %get-tuple-element.30.lhs, bf16[2048,128]{1,0:T(8,128)(2,1)S(1)} %get-tuple-element.31.rows0, f32[1,2048]{1,0:T(1,128)S(1)} %get-tuple-element.32.half_ref, f32[1,2048]{1,0:T(1,128)S(1)} %get-tuple-element.33.scale, ...), custom_call_target="tpu_custom_call" | custom-call | tf_op jit(solution)/shard_map/finish/pallas_call | solution.py:148
Async XLA Ops:
  0.0 5.5 %collective-permute-start.1 = (bf16[2048,128]{1,0:T(8,128)(2,1)}, bf16[2048,128]{1,0:T(8,128)(2,1)S(1)}, u32[]{:S(2)}, u32[]{:S(2)}) collective-permute-start(bf16[2048,128]{1,0:T(8,128)(2,1)} %own_rows.1), channel_id=1, source_target_pairs={{0,8},{8,0},{16,24},{24,16},{1,9},{9,1},{17,25},{25,17},{2,10},{10... | collective-permute-start | bytes 1572872 | tf_op jit(solution)/shard_map/ppermute | solution.py:17
  0.5 16.0 %collective-permute-start = (bf16[2048,128]{1,0:T(8,128)(2,1)}, bf16[2048,128]{1,0:T(8,128)(2,1)S(1)}, u32[]{:S(2)}, u32[]{:S(2)}) collective-permute-start(bf16[2048,128]{1,0:T(8,128)(2,1)} %own_rows.1), channel_id=1, source_target_pairs={{0,16},{8,24},{16,0},{24,8},{1,17},{9,25},{17,1},{25,9},{2,18},{10... | collective-permute-start | bytes 1572872 | tf_op jit(solution)/shard_map/ppermute | solution.py:17
  2.9 10.6 %collective-permute-start.4 = (bf16[64,1024]{1,0:T(8,128)(2,1)}, bf16[64,1024]{1,0:T(8,128)(2,1)S(1)}, u32[]{:S(2)}, u32[]{:S(2)}) collective-permute-start(bf16[64,1024]{1,0:T(8,128)(2,1)} %bitcast.4), channel_id=1, source_target_pairs={{0,4},{2,6},{4,0},{6,2},{1,5},{3,7},{5,1},{7,3},{8,12},{10,14},{12... | collective-permute-start | bytes 393224 | tf_op jit(solution)/shard_map/ppermute | solution.py:17
  5.5 8.0 %collective-permute-start.5 = (bf16[64,1024]{1,0:T(8,128)(2,1)}, bf16[64,1024]{1,0:T(8,128)(2,1)S(1)}, u32[]{:S(2)}, u32[]{:S(2)}) collective-permute-start(bf16[64,1024]{1,0:T(8,128)(2,1)} %bitcast.5), channel_id=1, source_target_pairs={{0,2},{2,0},{4,6},{6,4},{1,3},{3,1},{5,7},{7,5},{8,10},{10,8},{12,... | collective-permute-start | bytes 393224 | tf_op jit(solution)/shard_map/ppermute | solution.py:17
  7.1 10.5 %collective-permute-start.3 = (bf16[64,1024]{1,0:T(8,128)(2,1)}, bf16[64,1024]{1,0:T(8,128)(2,1)S(1)}, u32[]{:S(2)}, u32[]{:S(2)}) collective-permute-start(bf16[64,1024]{1,0:T(8,128)(2,1)} %bitcast.6), channel_id=1, source_target_pairs={{0,7},{1,6},{2,5},{3,4},{4,3},{5,2},{6,1},{7,0},{8,15},{9,14},{10,... | collective-permute-start | bytes 393224 | tf_op jit(solution)/shard_map/ppermute | solution.py:172
  8.6 9.0 %collective-permute-start.2 = (bf16[64,1024]{1,0:T(8,128)(2,1)}, bf16[64,1024]{1,0:T(8,128)(2,1)S(1)}, u32[]{:S(2)}, u32[]{:S(2)}) collective-permute-start(bf16[64,1024]{1,0:T(8,128)(2,1)} %bitcast.7), channel_id=1, source_target_pairs={{0,1},{1,0},{2,3},{3,2},{4,5},{5,4},{6,7},{7,6},{8,9},{9,8},{10,11... | collective-permute-start | bytes 393224 | tf_op jit(solution)/shard_map/ppermute | solution.py:17
  13.5 6.8 %collective-permute-start.6 = (bf16[64,1024]{1,0:T(8,128)(2,1)S(1)}, bf16[64,1024]{1,0:T(8,128)(2,1)S(1)}, u32[]{:S(2)}, u32[]{:S(2)}) collective-permute-start(bf16[64,1024]{1,0:T(8,128)(2,1)S(1)} %collective-permute-done.5.refs_0_), channel_id=1, source_target_pairs={{0,1},{1,0},{2,3},{3,2},{4,5},{5,4},{6,7},{7,6},{8,9},{9,8},{10,11... | collective-permute-start | bytes 393224 | tf_op jit(solution)/shard_map/ppermute | solution.py:17
  15.1 5.3 %collective-permute-start.7 = (bf16[64,1024]{1,0:T(8,128)(2,1)S(1)}, bf16[64,1024]{1,0:T(8,128)(2,1)S(1)}, u32[]{:S(2)}, u32[]{:S(2)}) collective-permute-start(bf16[64,1024]{1,0:T(8,128)(2,1)S(1)} %collective-permute-done.4.same), channel_id=1, source_target_pairs={{0,2},{2,0},{4,6},{6,4},{1,3},{3,1},{5,7},{7,5},{8,10},{10,8},{12,... | collective-permute-start | bytes 393224 | tf_op jit(solution)/shard_map/ppermute | solution.py:17
  16.4 6.1 %collective-permute-start.9 = (bf16[64,1024]{1,0:T(8,128)(2,1)S(1)}, bf16[64,1024]{1,0:T(8,128)(2,1)S(1)}, u32[]{:S(2)}, u32[]{:S(2)}) collective-permute-start(bf16[64,1024]{1,0:T(8,128)(2,1)S(1)} %collective-permute-done.4.same), channel_id=1, source_target_pairs={{0,1},{1,0},{2,3},{3,2},{4,5},{5,4},{6,7},{7,6},{8,9},{9,8},{10,11... | collective-permute-start | bytes 393224 | tf_op jit(solution)/shard_map/ppermute | solution.py:17
  17.6 5.7 %collective-permute-start.8 = (bf16[2048,128]{1,0:T(8,128)(2,1)S(1)}, bf16[2048,128]{1,0:T(8,128)(2,1)S(1)}, u32[]{:S(2)}, u32[]{:S(2)}) collective-permute-start(bf16[2048,128]{1,0:T(8,128)(2,1)S(1)} %collective-permute-done.refs_5_.far), channel_id=1, source_target_pairs={{0,8},{8,0},{16,24},{24,16},{1,9},{9,1},{17,25},{25,17},{2,10},{10... | collective-permute-start | bytes 1572872 | tf_op jit(solution)/shard_map/ppermute | solution.py:17

commit v6 on v5

--- a/solution.py
+++ b/solution.py
@@ -170,9 +170,9 @@
     one = swap(late, "col", n_col, 1)
     y0 = swap(late, "depth", n_depth, 1)
     y3 = lax.ppermute(late, ("col", "depth"), [(i, i ^ 7) for i in range(8)])
-    two, one = lax.optimization_barrier((two, one))
+    one, two = lax.optimization_barrier((one, two))
+    y1 = swap(one, "depth", n_depth, 1)
     three = swap(two, "col", n_col, 1)
-    y1 = swap(one, "depth", n_depth, 1)
     y2 = swap(two, "depth", n_depth, 1)
     far, y0, y3 = lax.optimization_barrier((far, y0, y3))
     farside = swap(far, "row", n_row, 1)

time: 27.9 us -> 27.9 us (level)
  no operation moved by 1% of the time
where the time goes in v6:
time: 27.9 us; the launch traced here: 27.8 us
  starting transfers between devices  13.1 us (47%)
  waiting for transfers between devices  7.33 us (26%)
  Pallas kernels  7.23 us (26%)
    ppermute x9, starting transfers between devices, swap(): return lax.ppermute(value, axis, [(i, i ^ bit) for i in range(size)])  11.6 us
    ppermute x9, waiting for transfers between devices, swap(): return lax.ppermute(value, axis, [(i, i ^ bit) for i in range(size)])  7.33 us
    pallas_call x1, Pallas kernels, finish(): pl.pallas_call(functools.partial(finish_kernel, cols=cols, tile=tile), in...  4.47 us
    pallas_call x1, Pallas kernels, prepare(): pl.pallas_call(functools.partial(prepare_kernel, width=8 * feats, step=25...  2.07 us
    ppermute x1, starting transfers between devices, per_device(): y3 = lax.ppermute(late, ('col', 'depth'), [(i, i ^ 7) for i in range(8)])  1.46 us
    pallas_call x1, Pallas kernels, turn(): pl.pallas_call(turn_kernel, in_specs=[SMEM] + [VMEM] * 3, out_specs=[VMEM...  0.69 us
  transfers between devices with their start and end apart: 10, of which 3 were waited for; matrix products, arithmetic and copies ran while one was open for 0% of the time, Pallas kernels for 10%

profile of v6, /device:TPU:0, one launch (start us, length us, event | category | flops | bytes accessed | tf_op | source)
XLA Modules:
  0.0 27.8 jit_solution(2679105620542633599)
XLA Ops:
  0.0 0.5 %collective-permute-start.1 = (bf16[2048,128]{1,0:T(8,128)(2,1)}, bf16[2048,128]{1,0:T(8,128)(2,1)S(1)}, u32[]{:S(2)}, u32[]{:S(2)}) collective-permute-start(bf16[2048,128]{1,0:T(8,128)(2,1)} %own_rows.1), channel_id=1, source_target_pairs={{0,8},{8,0},{16,24},{24,16},{1,9},{9,1},{17,25},{25,17},{2,10},{10... | collective-permute-start | bytes 1572872 | tf_op jit(solution)/shard_map/ppermute | solution.py:17
  0.5 2.5 %collective-permute-start = (bf16[2048,128]{1,0:T(8,128)(2,1)}, bf16[2048,128]{1,0:T(8,128)(2,1)S(1)}, u32[]{:S(2)}, u32[]{:S(2)}) collective-permute-start(bf16[2048,128]{1,0:T(8,128)(2,1)} %own_rows.1), channel_id=1, source_target_pairs={{0,16},{8,24},{16,0},{24,8},{1,17},{9,25},{17,1},{25,9},{2,18},{10... | collective-permute-start | bytes 1572872 | tf_op jit(solution)/shard_map/ppermute | solution.py:17
  2.9 2.6 %collective-permute-start.5 = (bf16[64,1024]{1,0:T(8,128)(2,1)}, bf16[64,1024]{1,0:T(8,128)(2,1)S(1)}, u32[]{:S(2)}, u32[]{:S(2)}) collective-permute-start(bf16[64,1024]{1,0:T(8,128)(2,1)} %bitcast.4), channel_id=1, source_target_pairs={{0,4},{2,6},{4,0},{6,2},{1,5},{3,7},{5,1},{7,3},{8,12},{10,14},{12... | collective-permute-start | bytes 393224 | tf_op jit(solution)/shard_map/ppermute | solution.py:17
  5.5 0.0 collective-permute-done.1.refs_4_.side
  5.5 1.6 %collective-permute-start.4 = (bf16[64,1024]{1,0:T(8,128)(2,1)}, bf16[64,1024]{1,0:T(8,128)(2,1)S(1)}, u32[]{:S(2)}, u32[]{:S(2)}) collective-permute-start(bf16[64,1024]{1,0:T(8,128)(2,1)} %bitcast.5), channel_id=1, source_target_pairs={{0,2},{2,0},{4,6},{6,4},{1,3},{3,1},{5,7},{7,5},{8,10},{10,8},{12,... | collective-permute-start | bytes 393224 | tf_op jit(solution)/shard_map/ppermute | solution.py:17
  7.1 1.5 %collective-permute-start.3 = (bf16[64,1024]{1,0:T(8,128)(2,1)}, bf16[64,1024]{1,0:T(8,128)(2,1)S(1)}, u32[]{:S(2)}, u32[]{:S(2)}) collective-permute-start(bf16[64,1024]{1,0:T(8,128)(2,1)} %bitcast.6), channel_id=1, source_target_pairs={{0,7},{1,6},{2,5},{3,4},{4,3},{5,2},{6,1},{7,0},{8,15},{9,14},{10,... | collective-permute-start | bytes 393224 | tf_op jit(solution)/shard_map/ppermute | solution.py:172
  8.6 0.5 %collective-permute-start.2 = (bf16[64,1024]{1,0:T(8,128)(2,1)}, bf16[64,1024]{1,0:T(8,128)(2,1)S(1)}, u32[]{:S(2)}, u32[]{:S(2)}) collective-permute-start(bf16[64,1024]{1,0:T(8,128)(2,1)} %bitcast.7), channel_id=1, source_target_pairs={{0,1},{1,0},{2,3},{3,2},{4,5},{5,4},{6,7},{7,6},{8,9},{9,8},{10,11... | collective-permute-start | bytes 393224 | tf_op jit(solution)/shard_map/ppermute | solution.py:17
  9.1 4.5 %collective-permute-done.5.same = bf16[64,1024]{1,0:T(8,128)(2,1)S(1)} collective-permute-done((bf16[64,1024]{1,0:T(8,128)(2,1)}, bf16[64,1024]{1,0:T(8,128)(2,1)S(1)}, u32[]{:S(2)}, u32[]{:S(2)}) %collective-permute-start.5) | collective-permute-done | bytes 131104 | tf_op jit(solution)/shard_map/ppermute | solution.py:17
  13.5 0.0 collective-permute-done.4.refs_0_
  13.5 1.5 %collective-permute-start.6 = (bf16[64,1024]{1,0:T(8,128)(2,1)S(1)}, bf16[64,1024]{1,0:T(8,128)(2,1)S(1)}, u32[]{:S(2)}, u32[]{:S(2)}) collective-permute-start(bf16[64,1024]{1,0:T(8,128)(2,1)S(1)} %collective-permute-done.4.refs_0_), channel_id=1, source_target_pairs={{0,1},{1,0},{2,3},{3,2},{4,5},{5,4},{6,7},{7,6},{8,9},{9,8},{10,11... | collective-permute-start | bytes 393224 | tf_op jit(solution)/shard_map/ppermute | solution.py:17
  15.1 1.4 %collective-permute-start.7 = (bf16[64,1024]{1,0:T(8,128)(2,1)S(1)}, bf16[64,1024]{1,0:T(8,128)(2,1)S(1)}, u32[]{:S(2)}, u32[]{:S(2)}) collective-permute-start(bf16[64,1024]{1,0:T(8,128)(2,1)S(1)} %collective-permute-done.5.same), channel_id=1, source_target_pairs={{0,2},{2,0},{4,6},{6,4},{1,3},{3,1},{5,7},{7,5},{8,10},{10,8},{12,... | collective-permute-start | bytes 393224 | tf_op jit(solution)/shard_map/ppermute | solution.py:17
  16.4 0.0 collective-permute-done.refs_5_.far
  16.4 1.1 %collective-permute-start.9 = (bf16[64,1024]{1,0:T(8,128)(2,1)S(1)}, bf16[64,1024]{1,0:T(8,128)(2,1)S(1)}, u32[]{:S(2)}, u32[]{:S(2)}) collective-permute-start(bf16[64,1024]{1,0:T(8,128)(2,1)S(1)} %collective-permute-done.5.same), channel_id=1, source_target_pairs={{0,1},{1,0},{2,3},{3,2},{4,5},{5,4},{6,7},{7,6},{8,9},{9,8},{10,11... | collective-permute-start | bytes 393224 | tf_op jit(solution)/shard_map/ppermute | solution.py:17
  17.5 0.1 pad_add_fusion.here
  17.6 0.0 collective-permute-done.3.refs_3_
  17.6 0.0 collective-permute-done.2.other
  17.6 0.0 collective-permute-start.8
  17.6 2.8 %collective-permute-done.6.refs_1_ = bf16[64,1024]{1,0:T(8,128)(2,1)S(1)} collective-permute-done((bf16[64,1024]{1,0:T(8,128)(2,1)S(1)}, bf16[64,1024]{1,0:T(8,128)(2,1)S(1)}, u32[]{:S(2)}, u32[]{:S(2)}) %collective-permute-start.6) | collective-permute-done | bytes 131104 | tf_op jit(solution)/shard_map/ppermute | solution.py:17
  20.4 0.0 collective-permute-done.7.refs_2_
  20.4 2.1 %prepare.1 = (bf16[4,1024,128]{2,1,0:T(8,128)(2,1)S(1)}, f32[1024,128]{1,0:T(8,128)S(1)}, bf16[2048,128]{1,0:T(8,128)(2,1)S(1)}, f32[1,2048]{1,0:T(1,128)S(1)}, f32[1,2048]{1,0:T(1,128)S(1)}) custom-call(s32[2]{0:T(128)S(1)} %pad_add_fusion.here, bf16[64,1024]{1,0:T(8,128)(2,1)} %bitcast.8, bf16[2048,128]{1,0:T(8,128)(2,1)} %own_rows.1, f32[1,2048]{1,0:T(1,128)} %bitcast.9, ...), custom_call_target="tpu_custom_call" | custom-call | tf_op jit(solution)/shard_map/prepare/pallas_call | solution.py:107
  22.5 0.1 collective-permute-done.9.other
  22.6 0.7 %turn.1 = (bf16[1024,128]{1,0:T(8,128)(2,1)S(1)}, f32[1024,128]{1,0:T(8,128)S(1)}) custom-call(s32[2]{0:T(128)S(1)} %pad_add_fusion.here, f32[1024,128]{1,0:T(8,128)S(1)} %get-tuple-element.34.squares, bf16[64,1024]{1,0:T(8,128)(2,1)S(1)} %collective-permute-done.5.same, bf16[64,1024]{1,0:T(8,128)(2,1)S(1)} %collective-permute-done.9.other), custom_call_target="tpu_custom_call" | custom-call | flops 10000000000 | bytes 4194304 | tf_op jit(solution)/shard_map/turn/pallas_call | solution.py:131
  23.3 0.0 collective-permute-done.8.farside
  23.3 4.5 %finish.1 = f32[1024,2048]{1,0:T(8,128)} custom-call(s32[2]{0:T(128)S(1)} %pad_add_fusion.here, bf16[4,1024,128]{2,1,0:T(8,128)(2,1)S(1)} %get-tuple-element.30.lhs, bf16[2048,128]{1,0:T(8,128)(2,1)S(1)} %get-tuple-element.31.rows0, f32[1,2048]{1,0:T(1,128)S(1)} %get-tuple-element.32.half_ref, f32[1,2048]{1,0:T(1,128)S(1)} %get-tuple-element.33.scale, ...), custom_call_target="tpu_custom_call" | custom-call | tf_op jit(solution)/shard_map/finish/pallas_call | solution.py:148
Async XLA Ops:
  0.0 5.5 %collective-permute-start.1 = (bf16[2048,128]{1,0:T(8,128)(2,1)}, bf16[2048,128]{1,0:T(8,128)(2,1)S(1)}, u32[]{:S(2)}, u32[]{:S(2)}) collective-permute-start(bf16[2048,128]{1,0:T(8,128)(2,1)} %own_rows.1), channel_id=1, source_target_pairs={{0,8},{8,0},{16,24},{24,16},{1,9},{9,1},{17,25},{25,17},{2,10},{10... | collective-permute-start | bytes 1572872 | tf_op jit(solution)/shard_map/ppermute | solution.py:17
  0.5 16.0 %collective-permute-start = (bf16[2048,128]{1,0:T(8,128)(2,1)}, bf16[2048,128]{1,0:T(8,128)(2,1)S(1)}, u32[]{:S(2)}, u32[]{:S(2)}) collective-permute-start(bf16[2048,128]{1,0:T(8,128)(2,1)} %own_rows.1), channel_id=1, source_target_pairs={{0,16},{8,24},{16,0},{24,8},{1,17},{9,25},{17,1},{25,9},{2,18},{10... | collective-permute-start | bytes 1572872 | tf_op jit(solution)/shard_map/ppermute | solution.py:17
  2.9 10.6 %collective-permute-start.5 = (bf16[64,1024]{1,0:T(8,128)(2,1)}, bf16[64,1024]{1,0:T(8,128)(2,1)S(1)}, u32[]{:S(2)}, u32[]{:S(2)}) collective-permute-start(bf16[64,1024]{1,0:T(8,128)(2,1)} %bitcast.4), channel_id=1, source_target_pairs={{0,4},{2,6},{4,0},{6,2},{1,5},{3,7},{5,1},{7,3},{8,12},{10,14},{12... | collective-permute-start | bytes 393224 | tf_op jit(solution)/shard_map/ppermute | solution.py:17
  5.5 8.0 %collective-permute-start.4 = (bf16[64,1024]{1,0:T(8,128)(2,1)}, bf16[64,1024]{1,0:T(8,128)(2,1)S(1)}, u32[]{:S(2)}, u32[]{:S(2)}) collective-permute-start(bf16[64,1024]{1,0:T(8,128)(2,1)} %bitcast.5), channel_id=1, source_target_pairs={{0,2},{2,0},{4,6},{6,4},{1,3},{3,1},{5,7},{7,5},{8,10},{10,8},{12,... | collective-permute-start | bytes 393224 | tf_op jit(solution)/shard_map/ppermute | solution.py:17
  7.1 10.5 %collective-permute-start.3 = (bf16[64,1024]{1,0:T(8,128)(2,1)}, bf16[64,1024]{1,0:T(8,128)(2,1)S(1)}, u32[]{:S(2)}, u32[]{:S(2)}) collective-permute-start(bf16[64,1024]{1,0:T(8,128)(2,1)} %bitcast.6), channel_id=1, source_target_pairs={{0,7},{1,6},{2,5},{3,4},{4,3},{5,2},{6,1},{7,0},{8,15},{9,14},{10,... | collective-permute-start | bytes 393224 | tf_op jit(solution)/shard_map/ppermute | solution.py:172
  8.6 9.0 %collective-permute-start.2 = (bf16[64,1024]{1,0:T(8,128)(2,1)}, bf16[64,1024]{1,0:T(8,128)(2,1)S(1)}, u32[]{:S(2)}, u32[]{:S(2)}) collective-permute-start(bf16[64,1024]{1,0:T(8,128)(2,1)} %bitcast.7), channel_id=1, source_target_pairs={{0,1},{1,0},{2,3},{3,2},{4,5},{5,4},{6,7},{7,6},{8,9},{9,8},{10,11... | collective-permute-start | bytes 393224 | tf_op jit(solution)/shard_map/ppermute | solution.py:17
  13.5 6.8 %collective-permute-start.6 = (bf16[64,1024]{1,0:T(8,128)(2,1)S(1)}, bf16[64,1024]{1,0:T(8,128)(2,1)S(1)}, u32[]{:S(2)}, u32[]{:S(2)}) collective-permute-start(bf16[64,1024]{1,0:T(8,128)(2,1)S(1)} %collective-permute-done.4.refs_0_), channel_id=1, source_target_pairs={{0,1},{1,0},{2,3},{3,2},{4,5},{5,4},{6,7},{7,6},{8,9},{9,8},{10,11... | collective-permute-start | bytes 393224 | tf_op jit(solution)/shard_map/ppermute | solution.py:17
  15.1 5.3 %collective-permute-start.7 = (bf16[64,1024]{1,0:T(8,128)(2,1)S(1)}, bf16[64,1024]{1,0:T(8,128)(2,1)S(1)}, u32[]{:S(2)}, u32[]{:S(2)}) collective-permute-start(bf16[64,1024]{1,0:T(8,128)(2,1)S(1)} %collective-permute-done.5.same), channel_id=1, source_target_pairs={{0,2},{2,0},{4,6},{6,4},{1,3},{3,1},{5,7},{7,5},{8,10},{10,8},{12,... | collective-permute-start | bytes 393224 | tf_op jit(solution)/shard_map/ppermute | solution.py:17
  16.4 6.1 %collective-permute-start.9 = (bf16[64,1024]{1,0:T(8,128)(2,1)S(1)}, bf16[64,1024]{1,0:T(8,128)(2,1)S(1)}, u32[]{:S(2)}, u32[]{:S(2)}) collective-permute-start(bf16[64,1024]{1,0:T(8,128)(2,1)S(1)} %collective-permute-done.5.same), channel_id=1, source_target_pairs={{0,1},{1,0},{2,3},{3,2},{4,5},{5,4},{6,7},{7,6},{8,9},{9,8},{10,11... | collective-permute-start | bytes 393224 | tf_op jit(solution)/shard_map/ppermute | solution.py:17
  17.6 5.7 %collective-permute-start.8 = (bf16[2048,128]{1,0:T(8,128)(2,1)S(1)}, bf16[2048,128]{1,0:T(8,128)(2,1)S(1)}, u32[]{:S(2)}, u32[]{:S(2)}) collective-permute-start(bf16[2048,128]{1,0:T(8,128)(2,1)S(1)} %collective-permute-done.refs_5_.far), channel_id=1, source_target_pairs={{0,8},{8,0},{16,24},{24,16},{1,9},{9,1},{17,25},{25,17},{2,10},{10... | collective-permute-start | bytes 1572872 | tf_op jit(solution)/shard_map/ppermute | solution.py:17
